TPU v7x, 32 devices: a whole 2x2x4 slice. The times are simulated.
32 devices in a mesh: groups: 2 (over y), dev: 8 (over z, x), sub: 2 (over core).
Axes of the slice: x: 2, y: 2, z: 4, core: 2. Of those that a mesh axis runs over, the one named last changes fastest.
Arguments:
- tokens: bfloat16 [2048, 2048], P(('groups', 'dev')), parts along dimension 0, may hold values from -6 to 6
- query_key_value: bfloat16 [2048, 3, 2048], P(('groups', 'dev'), None, 'sub'), parts along dimension 0, may hold values from -6 to 6
- out_weight: bfloat16 [2048, 2048], P('dev', 'sub'), may hold values from -0.125 to 0.125
- modulation: float32 [8, 2048], P('groups'), parts along dimension 0, may hold values from -3 to 3
- router_weight: bfloat16 [2048, 64], replicated, may hold values from -0.125 to 0.125
- expert_ids: int32 [2048, 4], P(('groups', 'dev')), parts along dimension 0, may hold values from 0 to 63, all different within a row; in each aligned block of 128 rows (0 to 127, 128 to 255, ...) at most 12 rows name the same one
- gate_up_weight: bfloat16 [128, 2, 2048, 384], P('dev', None, None, 'sub'), may hold values from -0.125 to 0.125
- down_weight: bfloat16 [128, 384, 2048], P('dev', None, 'sub'), may hold values from -0.21875 to 0.21875
Outputs:
- block_out: bfloat16 [2048, 2048], P(('groups', 'dev'), 'sub'), parts along dimension 0
There are 2 independent parts, one for each index of `groups`. A program takes and returns all parts, laid end to end along the dimension named above; an argument that names none is the same for every part. Nothing has to cross between parts.
Inputs may be any that keep to these rules, and one draw needn't show every extreme that they name: `expert_ids`: each token names 4 different experts. Within each aligned block of 128 rows no expert is named by more than 12 rows, a bound that some block reaches.
All inputs are finite; a program needn't handle non-finite values.
Results may differ from a plain program's by a relative error of at most 0.008.
Values may be sent and summed in bfloat16 or wider, within the bound.
A program may use at most 128 MiB of HBM per device.

v0:
```python
import functools
import math

import jax
import jax.numpy as jnp
from jax import lax
from jax.experimental import pallas as pl
from jax.experimental.pallas import tpu as pltpu
from jax.sharding import PartitionSpec as P

HEAD = 128
CAP = 12


EPS = 1e-06
NEG = -1e30


def extended(cells, sides, width):
    for axis, dim in sides:
        count = lax.axis_size(axis)
        ends = count - 1
        head = lax.slice_in_dim(cells, 0, width, axis=dim)
        tail = lax.slice_in_dim(cells, cells.shape[dim] - width, cells.shape[dim], axis=dim)
        cells = jnp.concatenate(
            [
                lax.ppermute(tail, axis, [(i, (i + 1) % count) for i in range(ends)]),
                cells,
                lax.ppermute(head, axis, [((i + 1) % count, i) for i in range(ends)]),
            ],
            axis=dim,
        )
    return cells


def window_attention(query, keys, values, index, total):
    count = query.shape[0]
    rows = jnp.arange(count, dtype=jnp.int32)[:, None]
    cols = jnp.arange(3 * count, dtype=jnp.int32)[None, :] - count
    place = index * count + cols
    allowed = (jnp.abs(cols - rows) <= count) & (place >= 0) & (place < total)
    scores = jnp.einsum(
        "qhd,khd->hqk", query, keys, preferred_element_type=jnp.float32
    ) / math.sqrt(query.shape[2])
    scores = jnp.where(allowed[None], scores, NEG)
    top = jnp.max(scores, -1, keepdims=True)
    weight = jnp.exp(scores - top)
    weight = (weight / jnp.sum(weight, -1, keepdims=True)).astype(jnp.bfloat16)
    mixed = jnp.einsum("hqk,khd->qhd", weight, values, preferred_element_type=jnp.float32)
    return mixed.astype(jnp.bfloat16)


def normalize(state, modulation):
    scale = lax.rsqrt(jnp.mean(state * state, -1, keepdims=True) + EPS)
    return (state * scale * (1.0 + modulation[2]) + modulation[1]).astype(jnp.bfloat16)


def route(normed, router_weight, expert_ids):
    logits = jnp.dot(normed, router_weight, preferred_element_type=jnp.float32)
    experts = router_weight.shape[1]
    match = expert_ids[:, :, None] == jnp.arange(experts, dtype=jnp.int32)[None, None, :]
    picked = jnp.sum(jnp.where(match, logits[:, None, :], 0.0), -1)
    lifted = jax.nn.sigmoid(picked)
    return lifted / jnp.sum(lifted, -1, keepdims=True)


LANES = 128
SLOT = 16
COLS = 2
VMEM_BYTES = 66 * 1000 * 1000
MESH = pl.DeviceIdType.MESH


def expert_kernel(
    devices, weight_copies,
    normed, meta, state, modulation, gate_up, down,
    out,
    tok, disp, gu, dn, hid_own, hid_other, got_meta, pick, slot_gate, got_x, got_up, got_down, acc,
    meta_s, meta_r, ag_s, ag_r, core_r, hid_s, hid_r,
    x_s, x_r, up_s, up_r, down_s, down_r,
):
    me = lax.axis_index("dev")
    part = lax.axis_index("sub")
    other = 1 - part
    z = me // COLS
    x = me % COLS
    across = z * COLS + (1 - x)
    lines = devices // COLS
    count, width = normed.shape
    half = width // 2
    halves = gate_up.shape[0]
    local = halves // 2
    hidden = gate_up.shape[2]
    slots = local * SLOT

    def remote(src, dst, send, recv, where):
        return pltpu.make_async_remote_copy(
            src_ref=src, dst_ref=dst, send_sem=send, recv_sem=recv,
            device_id=where, device_id_type=MESH,
        )

    def block(s, way, where, src=None):
        dst = tok.at[part, s]
        recv = core_r.at[s] if way == 3 else ag_r.at[s]
        return remote(dst if src is None else src, dst, ag_s.at[s, way], recv, where)

    up_to = {"dev": jnp.minimum(me + COLS, devices - 1)}
    down_to = {"dev": jnp.maximum(me - COLS, 0)}
    x_to = {"dev": across}
    core_to = {"sub": other}
    not_top = z < lines - 1
    not_bottom = z > 0
    mine = normed.at[:, pl.ds(pl.multiple_of(part * half, LANES), half)]

    def meta_copy(step):
        target = (me + step) % devices
        return remote(
            meta.at[pl.ds(pl.multiple_of(target * local, local), local)], got_meta.at[me],
            meta_s.at[step - 1], meta_r.at[me], {"dev": target},
        )

    for step in range(1, devices):
        meta_copy(step).start()

    @pl.when(not_top)
    def _():
        block(me, 0, up_to, mine).start()

    @pl.when(not_bottom)
    def _():
        block(me, 1, down_to, mine).start()

    block(me, 2, x_to, mine).start()

    before = (
        lax.broadcasted_iota(jnp.int32, (count, count), 0)
        < lax.broadcasted_iota(jnp.int32, (count, count), 1)
    ).astype(jnp.float32).astype(jnp.bfloat16)
    place = lax.broadcasted_iota(jnp.int32, (local, SLOT, count), 1).astype(jnp.float32)

    def routing(s, gate):
        chosen = jnp.where(gate > 0.0, 1.0, 0.0)
        rank = jnp.dot(chosen.astype(jnp.bfloat16), before, preferred_element_type=jnp.float32)
        rank = jnp.where(gate > 0.0, rank, -1.0)
        hit = jnp.broadcast_to(rank[:, None, :], place.shape) == place
        pick[s] = jnp.where(hit, 1.0, 0.0).reshape(slots, count).astype(jnp.bfloat16)
        value = jnp.where(hit, jnp.broadcast_to(gate[:, None, :], place.shape), 0.0)
        value = jnp.sum(value, -1, keepdims=True)
        slot_gate[:, pl.ds(pl.multiple_of(s * SLOT, SLOT), SLOT), :] = jnp.broadcast_to(
            value, (local, SLOT, LANES)
        )

    def dispatch(s, h, rows):
        moved = jnp.dot(pick[s], rows, preferred_element_type=jnp.float32)
        disp[h, :, pl.ds(pl.multiple_of(s * SLOT, SLOT), SLOT), :] = moved.astype(
            jnp.bfloat16
        ).reshape(local, SLOT, half)

    routing(me, meta[pl.ds(pl.multiple_of(me * local, local), local)])
    dispatch(me, 0, normed[:, :half])
    dispatch(me, 1, normed[:, half:])
    for step in range(1, devices):
        s = (me + step) % devices
        remote(
            meta.at[pl.ds(0, local)], got_meta.at[s], meta_s.at[0], meta_r.at[s], {"dev": s}
        ).wait_recv()
        routing(s, got_meta[s])

    def arrive(s):
        block(s, 2, x_to).wait_recv()

    def from_line(zz, way, where, more):
        s = zz * COLS + x
        arrive(s)

        @pl.when(more)
        def _():
            block(s, way, where).start()

        block(s, 2, x_to).start()
        block(s, 3, core_to).start()
        dispatch(s, part, tok[part, s])

    def from_across(zz):
        s = zz * COLS + (1 - x)
        arrive(s)
        block(s, 3, core_to).start()
        dispatch(s, part, tok[part, s])

    def from_core(s):
        remote(tok.at[other, s], tok.at[other, s], ag_s.at[s, 3], core_r.at[s], core_to).wait_recv()
        dispatch(s, other, tok[other, s])

    def both(d, act):
        @pl.when(z - d >= 0)
        def _():
            act(z - d, True)

        @pl.when(z + d < lines)
        def _():
            act(z + d, False)

    for d in range(1, lines):
        both(d, lambda zz, low: from_line(
            zz, 0 if low else 1, up_to if low else down_to, not_top if low else not_bottom
        ))
        if d == 1:
            from_across(z)
        else:
            both(d - 1, lambda zz, low: from_core(zz * COLS + x))
    both(lines - 1, lambda zz, low: from_core(zz * COLS + x))
    from_core(across)
    for d in range(1, lines):
        both(d, lambda zz, low: from_across(zz))
        if d > 1:
            both(d - 1, lambda zz, low: from_core(zz * COLS + (1 - x)))
    both(lines - 1, lambda zz, low: from_core(zz * COLS + (1 - x)))

    @pl.when(not_top)
    def _():
        block(me, 0, up_to, mine).wait_send()

    @pl.when(not_bottom)
    def _():
        block(me, 1, down_to, mine).wait_send()

    block(me, 2, x_to, mine).wait_send()
    for d in range(1, lines):

        def sent(zz, low):
            s = zz * COLS + x

            @pl.when(not_top if low else not_bottom)
            def _():
                block(s, 0 if low else 1, up_to).wait_send()

            block(s, 2, x_to).wait_send()
            block(s, 3, core_to).wait_send()
            block(zz * COLS + (1 - x), 3, core_to).wait_send()

        both(d, sent)
    block(across, 3, core_to).wait_send()

    def hid_copy(h):
        return remote(hid_own.at[h], hid_other.at[h], hid_s.at[h], hid_r.at[h], core_to)

    def across_rows(left, right):
        return lax.dot_general(
            left, right, (((1,), (1,)), ((), ())), preferred_element_type=jnp.float32
        )

    def raise_expert(e):
        low, high = disp[0, e], disp[1, e]
        for b in range(2):
            h = 2 * e + b
            weight_copies(h)[0].wait()

            def product(g):
                return across_rows(low, gu[h, g, :, :half]) + across_rows(high, gu[h, g, :, half:])

            gate = product(0)
            hid_own[h] = (gate * jax.nn.sigmoid(gate) * product(1)).astype(jnp.bfloat16)
            hid_copy(h).start()

    def lower_expert(e):
        total = None
        for b in range(2):
            h = 2 * e + b
            weight_copies(h)[1].wait()
            hid_copy(h).wait_recv()
            first = dn[h, pl.ds(pl.multiple_of(part * hidden, SLOT), hidden), :]
            second = dn[h, pl.ds(pl.multiple_of(other * hidden, SLOT), hidden), :]
            piece = jnp.dot(hid_own[h], first, preferred_element_type=jnp.float32) + jnp.dot(
                hid_other[h], second, preferred_element_type=jnp.float32
            )
            piece = piece.astype(jnp.bfloat16).astype(jnp.float32)
            total = piece if total is None else total + piece
        gain = slot_gate[e][:, :1]
        disp[0, e] = (total * gain).astype(jnp.bfloat16)

    raise_expert(0)

    def step_expert(e, carry):
        raise_expert(e)
        lower_expert(e - 1)
        return carry

    lax.fori_loop(1, local, step_expert, 0)
    lower_expert(local - 1)

    def combine(s):
        rows = disp[0, :, pl.ds(pl.multiple_of(s * SLOT, SLOT), SLOT), :].reshape(slots, half)
        return lax.dot_general(
            pick[s], rows, (((0,), (0,)), ((), ())), preferred_element_type=jnp.float32
        )

    def x_copy(zz):
        return remote(
            tok.at[0, zz * COLS + (1 - x)], got_x.at[zz], x_s.at[zz], x_r.at[zz], x_to
        )

    def line_copy(zz, low):
        if low:
            return remote(tok.at[1, zz], got_down.at[zz], down_s.at[zz], down_r.at[zz], down_to)
        return remote(tok.at[1, zz], got_up.at[zz], up_s.at[zz], up_r.at[zz], up_to)

    def give_across(zz, low):
        s = zz * COLS + (1 - x)
        tok[0, s] = combine(s).astype(jnp.bfloat16)
        x_copy(zz).start()

    def add_line(zz, low):
        line_copy(zz, low).wait_recv()
        acc[...] += (got_down if low else got_up)[zz].astype(jnp.float32)

    def gather_here(zz):
        acc[...] = combine(zz * COLS + x)
        x_copy(zz).wait_recv()
        acc[...] += got_x[zz].astype(jnp.float32)

    def pass_on(zz, low):
        gather_here(zz)

        @pl.when(not_top if low else not_bottom)
        def _():
            add_line(zz, low)

        tok[1, zz] = acc[...].astype(jnp.bfloat16)
        line_copy(zz, low).start()

    for d in range(lines - 1, 0, -1):
        both(d, give_across)
    give_across(z, False)
    for d in range(lines - 1, 0, -1):
        both(d, pass_on)
    gather_here(z)

    @pl.when(not_bottom)
    def _():
        add_line(z, False)

    @pl.when(not_top)
    def _():
        add_line(z, True)

    own = pl.ds(pl.multiple_of(part * half, LANES), half)
    out[...] = (state[:, own] + (1.0 + modulation[3:4, own]) * acc[...]).astype(out.dtype)

    for d in range(1, lines):

        def drained(zz, low):
            line_copy(zz, low).wait_send()
            x_copy(zz).wait_send()

        both(d, drained)
    x_copy(z).wait_send()
    for step in range(1, devices):
        meta_copy(step).wait_send()

    def hid_drain(h, carry):
        hid_copy(h).wait_send()
        return carry

    lax.fori_loop(0, halves, hid_drain, 0)


def front_kernel(
    devices, start_weights,
    sources, held, own_sem,
    normed, state, meta,
    near, wide, mixed, mine_out, their_out,
    near_s, near_r, far_s, far_r, ag_s, ag_r, y_r, sum_s, sum_r,
):
    packed_hbm, weight_hbm = sources[1], sources[2]
    tokens, packed, weight, modulation, router, ids = held

    def own_copy(i):
        return pltpu.make_async_copy(sources[i], held[i], own_sem.at[i])

    for i in (1, 2, 0, 3, 4, 5):
        own_copy(i).start()
    me = lax.axis_index("dev")
    part = lax.axis_index("sub")
    group = lax.axis_index("groups")
    z = me // COLS
    x = me % COLS
    across = z * COLS + (1 - x)
    lines = devices // COLS
    count, width = tokens.shape
    shard = weight.shape[0]
    extra = shard * 3 // 8 // SLOT * SLOT
    main = shard - extra
    not_top = z < lines - 1
    not_bottom = z > 0
    up_to = {"dev": jnp.minimum(me + COLS, devices - 1)}
    down_to = {"dev": jnp.maximum(me - COLS, 0)}
    x_to = {"dev": across}
    y_to = {"groups": 1 - group}
    core_to = {"sub": 1 - part}

    barrier = pltpu.get_barrier_semaphore()
    for step in range(1, devices):
        pl.semaphore_signal(
            barrier, inc=1, device_id={"dev": (me + step) % devices}, device_id_type=MESH
        )
    pl.semaphore_signal(barrier, inc=1, device_id=core_to, device_id_type=MESH)
    pl.semaphore_signal(barrier, inc=1, device_id=y_to, device_id_type=MESH)
    pl.semaphore_wait(barrier, devices + 1)

    def remote(src, dst, send, recv, where):
        return pltpu.make_async_remote_copy(
            src_ref=src, dst_ref=dst, send_sem=send, recv_sem=recv,
            device_id=where, device_id_type=MESH,
        )

    def near_copy(i):
        return remote(packed_hbm.at[1 + i], near.at[x, i], near_s.at[i], near_r.at[i], x_to)

    def far_copy(i, where):
        return remote(near.at[1 - x, i], near.at[x, i], far_s.at[i], far_r.at[i], where)

    def piece(s, way, where, src=None):
        start, size = (main, extra) if way == 3 else (extra, main)
        dst = wide.at[s, pl.ds(pl.multiple_of(group * start, SLOT), size)]
        recv = y_r.at[s] if way == 3 else ag_r.at[s]
        return remote(dst if src is None else src, dst, ag_s.at[s, way], recv, where)

    far_up = (x == 0) & not_top
    far_down = (x == 1) & not_bottom
    have_far = ((x == 0) & not_bottom) | ((x == 1) & not_top)
    mine = weight_hbm.at[pl.ds(pl.multiple_of(group * extra, SLOT), main)]

    for i in range(2):
        near_copy(i).start()

    @pl.when(not_top)
    def _():
        piece(me, 0, up_to, mine).start()

    @pl.when(not_bottom)
    def _():
        piece(me, 1, down_to, mine).start()

    piece(me, 2, x_to, mine).start()
    start_weights()

    @pl.when(jnp.logical_not(have_far))
    def _():
        near[x] = jnp.zeros_like(near[x])

    for i in range(2):
        near_copy(i).wait_recv()

        @pl.when(far_up)
        def _():
            far_copy(i, up_to).start()

        @pl.when(far_down)
        def _():
            far_copy(i, down_to).start()

    def both(d, act):
        @pl.when(z - d >= 0)
        def _():
            act(z - d, True)

        @pl.when(z + d < lines)
        def _():
            act(z + d, False)

    def project(s, block):
        mine_out[s] = lax.dot_general(
            mixed[...], block, (((1,), (1,)), ((), ())), preferred_element_type=jnp.float32
        )
        sum_copy(s).start()

    def sum_copy(s):
        return remote(mine_out.at[s], their_out.at[s], sum_s.at[s], sum_r.at[s], core_to)

    def take_line(zz, low):
        s = zz * COLS + x
        piece(s, 2, x_to).wait_recv()

        @pl.when(not_top if low else not_bottom)
        def _():
            piece(s, 0 if low else 1, up_to if low else down_to).start()

        piece(s, 2, x_to).start()
        piece(s, 3, y_to).start()

    def take_across(zz, low):
        s = zz * COLS + (1 - x)
        piece(s, 2, x_to).wait_recv()
        piece(s, 3, y_to).start()

    def take_y(s):
        dst = wide.at[s, pl.ds(pl.multiple_of((1 - group) * main, SLOT), extra)]
        remote(dst, dst, ag_s.at[s, 3], y_r.at[s], y_to).wait_recv()
        project(s, wide[s])

    def line_y(zz, low):
        take_y(zz * COLS + x)

    def across_y(zz, low):
        take_y(zz * COLS + (1 - x))

    both(1, take_line)
    take_across(z, False)
    for d in range(2, min(3, lines)):
        both(d, take_line)
    for i in range(6):
        own_copy(i).wait()

    @pl.when(have_far)
    def _():
        for i in range(2):
            far_copy(i, x_to).wait_recv()

    row = lax.broadcasted_iota(jnp.int32, (count, count), 0)
    col = lax.broadcasted_iota(jnp.int32, (count, count), 1)
    see_before = (col >= row) & (me > 0)
    see_after = (col <= row) & (me < devices - 1)
    for h in range(mixed.shape[1] // HEAD):
        lanes = slice(h * HEAD, (h + 1) * HEAD)
        query = packed[0, :, lanes]

        def score(keys):
            return lax.dot_general(
                query, keys, (((1,), (1,)), ((), ())), preferred_element_type=jnp.float32
            ) / math.sqrt(HEAD)

        scores = jnp.concatenate(
            [
                jnp.where(see_before, score(near[0, 0, :, lanes]), NEG),
                score(packed[1, :, lanes]),
                jnp.where(see_after, score(near[1, 0, :, lanes]), NEG),
            ],
            axis=1,
        )
        top = jnp.max(scores, -1, keepdims=True)
        share = jnp.exp(scores - top)
        share = (share / jnp.sum(share, -1, keepdims=True)).astype(jnp.bfloat16)
        values = jnp.concatenate(
            [near[0, 1, :, lanes], packed[2, :, lanes], near[1, 1, :, lanes]], axis=0
        )
        mixed[:, lanes] = jnp.dot(
            share, values, preferred_element_type=jnp.float32
        ).astype(jnp.bfloat16)

    project(me, weight[...])
    for d in range(3, lines):
        both(d, take_line)
    for d in range(1, lines):
        both(d, line_y)
        both(d, take_across)
        if d == 1:
            take_y(across)
    for d in range(1, lines):
        both(d, across_y)

    square = jnp.zeros((count, 1), jnp.float32)
    for s in range(devices):
        sum_copy(s).wait_recv()
        lanes = slice(s * shard, (s + 1) * shard)
        value = tokens[:, lanes].astype(jnp.float32) + (1.0 + modulation[0:1, lanes]) * (
            mine_out[s] + their_out[s]
        )
        state[:, lanes] = value
        square = square + jnp.sum(value * value, -1, keepdims=True)
    scale = lax.rsqrt(square / width + EPS)
    for s in range(devices):
        lanes = slice(s * shard, (s + 1) * shard)
        normed[:, lanes] = (
            state[:, lanes] * scale * (1.0 + modulation[2:3, lanes]) + modulation[1:2, lanes]
        ).astype(jnp.bfloat16)
    logits = lax.dot_general(
        router[...], normed[...], (((1,), (1,)), ((), ())), preferred_element_type=jnp.float32
    )
    name = lax.broadcasted_iota(jnp.int32, logits.shape, 0)
    named = name == ids[0:1]
    for k in range(1, ids.shape[0]):
        named = named | (name == ids[k:k + 1])
    lifted = jnp.where(named, jax.nn.sigmoid(logits), 0.0)
    meta[...] = lifted / jnp.sum(lifted, 0, keepdims=True)

    for i in range(2):
        near_copy(i).wait_send()

        @pl.when(far_up | far_down)
        def _():
            far_copy(i, x_to).wait_send()

    @pl.when(not_top)
    def _():
        piece(me, 0, up_to, mine).wait_send()

    @pl.when(not_bottom)
    def _():
        piece(me, 1, down_to, mine).wait_send()

    piece(me, 2, x_to, mine).wait_send()
    piece(across, 3, y_to).wait_send()
    for d in range(1, lines):

        def sent(zz, low):
            s = zz * COLS + x

            @pl.when(not_top if low else not_bottom)
            def _():
                piece(s, 0 if low else 1, up_to).wait_send()

            piece(s, 2, x_to).wait_send()
            piece(s, 3, y_to).wait_send()
            piece(zz * COLS + (1 - x), 3, y_to).wait_send()

        both(d, sent)
    for s in range(devices):
        sum_copy(s).wait_send()


def block_kernel(devices, *refs):
    sources, gate_up, down, out = refs[:6], refs[6], refs[7], refs[8]
    held, normed, state, meta = refs[9:15], refs[15], refs[16], refs[17]
    front_buffers, expert_buffers = refs[18:23], refs[23:36]
    own_sem, gu_sem, dn_sem = refs[36:39]
    front_sems, expert_sems = refs[39:48], refs[48:]
    gu, dn = expert_buffers[2:4]
    halves = gate_up.shape[0]

    def weight_copies(h):
        return (
            pltpu.make_async_copy(gate_up.at[h], gu.at[h], gu_sem.at[h]),
            pltpu.make_async_copy(down.at[h], dn.at[h], dn_sem.at[h]),
        )

    def start_weights():
        def one(h, carry):
            for copy in weight_copies(h):
                copy.start()
            return carry

        lax.fori_loop(0, halves, one, 0)

    front_kernel(
        devices, start_weights, sources, held, own_sem, normed, state, meta,
        *front_buffers, *front_sems,
    )
    expert_kernel(
        devices, weight_copies, normed, meta, state, held[3], gate_up, down, out,
        *expert_buffers, *expert_sems,
    )


def block_call(
    tokens, query_key_value, out_weight, modulation, router_weight, expert_ids,
    gate_up_weight, down_weight,
):
    devices = lax.axis_size("dev")
    count, width = tokens.shape
    half = down_weight.shape[2]
    halves = gate_up_weight.shape[0]
    local = halves // 2
    gate_up_weight = gate_up_weight.swapaxes(2, 3)
    hidden = gate_up_weight.shape[2]
    lines = devices // COLS
    rows = devices * SLOT
    shard = out_weight.shape[0]
    own = (
        tokens, query_key_value.transpose(1, 0, 2), out_weight, modulation,
        router_weight.T, expert_ids.T,
    )
    hbm = pl.BlockSpec(memory_space=pl.ANY)
    dma = pltpu.SemaphoreType.DMA
    return pl.pallas_call(
        functools.partial(block_kernel, devices),
        out_shape=jax.ShapeDtypeStruct((count, half), jnp.bfloat16),
        in_specs=[hbm] * 8,
        out_specs=pl.BlockSpec(memory_space=pltpu.VMEM),
        scratch_shapes=[
            *[pltpu.VMEM(array.shape, array.dtype) for array in own],
            pltpu.VMEM((count, width), jnp.bfloat16),
            pltpu.VMEM((count, width), jnp.float32),
            pltpu.VMEM((router_weight.shape[1], count), jnp.float32),
            pltpu.VMEM((2, 2, count, half), jnp.bfloat16),
            pltpu.VMEM((devices, shard, half), jnp.bfloat16),
            pltpu.VMEM((count, half), jnp.bfloat16),
            pltpu.VMEM((devices, count, shard), jnp.float32),
            pltpu.VMEM((devices, count, shard), jnp.float32),
            pltpu.VMEM((2, devices, count, half), jnp.bfloat16),
            pltpu.VMEM((2, local, rows, half), jnp.bfloat16),
            pltpu.VMEM(gate_up_weight.shape, jnp.bfloat16),
            pltpu.VMEM(down_weight.shape, jnp.bfloat16),
            pltpu.VMEM((halves, rows, hidden), jnp.bfloat16),
            pltpu.VMEM((halves, rows, hidden), jnp.bfloat16),
            pltpu.VMEM((devices, local, count), jnp.float32),
            pltpu.VMEM((devices, local * SLOT, count), jnp.bfloat16),
            pltpu.VMEM((local, rows, LANES), jnp.float32),
            pltpu.VMEM((lines, count, half), jnp.bfloat16),
            pltpu.VMEM((lines, count, half), jnp.bfloat16),
            pltpu.VMEM((lines, count, half), jnp.bfloat16),
            pltpu.VMEM((count, half), jnp.float32),
            dma((6,)), dma((halves,)), dma((halves,)),
            dma((2,)), dma((2,)), dma((2,)), dma((2,)),
            dma((devices, 4)), dma((devices,)), dma((devices,)),
            dma((devices,)), dma((devices,)),
            dma((devices,)), dma((devices,)), dma((devices, 4)), dma((devices,)), dma((devices,)),
            dma((halves,)), dma((halves,)),
            dma((lines,)), dma((lines,)), dma((lines,)), dma((lines,)), dma((lines,)), dma((lines,)),
        ],
        compiler_params=pltpu.CompilerParams(
            collective_id=1, has_side_effects=True, vmem_limit_bytes=VMEM_BYTES
        ),
    )(*own, gate_up_weight, down_weight)


def body(
    tokens,
    query_key_value,
    out_weight,
    modulation,
    router_weight,
    expert_ids,
    gate_up_weight,
    down_weight,
):
    count = tokens.shape[0]
    width = tokens.shape[1]
    parts = lax.axis_size("sub")
    part = lax.axis_index("sub")
    position = lax.axis_index("dev")
    devices = lax.axis_size("dev")
    total = count * devices
    local_width = query_key_value.shape[2]
    weight_bytes = 2 * (gate_up_weight.size + down_weight.size)
    token_bytes = 12 * devices * count * width
    fits = weight_bytes + token_bytes < VMEM_BYTES and CAP <= SLOT
    paired = parts == 2 and lax.axis_size("groups") == 2 and devices % COLS == 0
    tiled = out_weight.shape[0] % (2 * LANES) == 0 and count == LANES
    if fits and paired and tiled:
        return block_call(
            tokens, query_key_value, out_weight, modulation, router_weight, expert_ids,
            gate_up_weight, down_weight,
        )
    heads_here = local_width // HEAD
    query = query_key_value[:, 0].reshape(count, heads_here, HEAD)
    pair = query_key_value[:, 1:]
    near = extended(pair, (("dev", 0),), count)
    keys = near[:, 0].reshape(3 * count, heads_here, HEAD)
    values = near[:, 1].reshape(3 * count, heads_here, HEAD)
    mixed = window_attention(query, keys, values, position, total).reshape(count, local_width)
    partial_proj = lax.dot_general(
        mixed,
        lax.all_gather(out_weight, "dev", axis=0, tiled=True),
        (((1,), (1,)), ((), ())),
        preferred_element_type=jnp.float32,
    )
    proj = lax.psum(partial_proj, "sub")
    state = tokens.astype(jnp.float32) + (1.0 + modulation[0]) * proj
    normed = normalize(state, modulation)
    gates = route(normed, router_weight, expert_ids)
    experts = router_weight.shape[1]
    topk = expert_ids.shape[1]
    flat = expert_ids.reshape(-1)
    picks = flat.shape[0]
    onehot = (flat[:, None] == jnp.arange(experts, dtype=jnp.int32)[None, :]).astype(jnp.int32)
    rank = jnp.sum((jnp.cumsum(onehot, 0) - 1) * onehot, 1)
    target = flat * CAP + rank
    hit = target[None, :] == jnp.arange(experts * CAP, dtype=jnp.int32)[:, None]
    filled = jnp.any(hit, 1)
    anchor = jnp.sum(jnp.where(hit, jnp.arange(picks, dtype=jnp.int32)[None, :], 0), 1) // topk
    slice_width = width // parts
    sent = lax.dynamic_slice_in_dim(normed, part * slice_width, slice_width, 1)
    sent_width = sent.shape[1]
    rows_out = jnp.where(filled[:, None], sent[anchor], jnp.zeros((), jnp.bfloat16))
    halves_here = gate_up_weight.shape[0]
    doubled = jnp.broadcast_to(
        rows_out.reshape(experts, 1, CAP, sent_width), (experts, 2, CAP, sent_width)
    )
    outgoing = doubled.reshape(devices, halves_here, CAP, sent_width)
    up_form = "sxcd,xgdf->sxcgf"
    down_form = "sxcf,xfd->sxcd"
    incoming = lax.all_to_all(outgoing, "dev", split_axis=0, concat_axis=0, tiled=True)
    both = jnp.einsum(
        up_form,
        lax.all_gather(incoming, "sub", axis=3, tiled=True),
        gate_up_weight,
        preferred_element_type=jnp.float32,
    )
    hidden = (jax.nn.silu(both[..., 0, :]) * both[..., 1, :]).astype(jnp.bfloat16)
    gathered = lax.all_gather(hidden, "sub", axis=hidden.ndim - 1, tiled=True)
    result = jnp.einsum(down_form, gathered, down_weight, preferred_element_type=jnp.float32)
    returned = lax.all_to_all(
        result.astype(jnp.bfloat16), "dev", split_axis=0, concat_axis=0, tiled=True
    )
    own_width = returned.shape[-1]
    arranged = returned.reshape(experts, 2, CAP, own_width)
    answers = arranged[flat, :, rank, :].reshape(count, topk, 2, own_width).astype(jnp.float32)
    combined = answers[:, :, 0] + answers[:, :, 1]
    routed = jnp.einsum("tk,tkd->td", gates, combined)
    own = lax.dynamic_slice_in_dim(state, part * slice_width, slice_width, 1)
    lift = lax.dynamic_slice_in_dim(modulation[3], part * slice_width, slice_width, 0)
    return (own + (1.0 + lift) * routed).astype(jnp.bfloat16)


def solution(mesh):
    return jax.shard_map(
        body,
        mesh=mesh,
        in_specs=(
            P(("groups", "dev"), None),
            P(("groups", "dev"), None, "sub"),
            P("dev", "sub"),
            P("groups", None),
            P(),
            P(("groups", "dev"), None),
            P("dev", None, None, "sub"),
            P("dev", None, "sub"),
        ),
        out_specs=P(("groups", "dev"), "sub"),
        check_vma=False,
    )
```

profile of v0, /device:TPU:0, one launch (start us, length us, event | category | flops | bytes accessed | tf_op | source)
XLA Modules:
  0.0 136.2 jit_solution(1283036575364866195)
XLA Ops:
  0.0 134.5 %shard_map.82 = bf16[128,1024]{1,0:T(8,128)(2,1)} custom-call(bf16[128,2048]{1,0:T(8,128)(2,1)} %refs_0_.1, bf16[3,128,1024]{2,1,0:T(8,128)(2,1)} %bitcast.5, bf16[256,1024]{1,0:T(8,128)(2,1)} %refs_2_.1, f32[4,2048]{1,0:T(4,128)} %refs_3_.1, bf16[64,2048]{1,0:T(8,128)(2,1)} %bitcast.6, s32[4,128]{1,0:T(4,128)} %bitcast.7, ...), custom_call_target="tpu_custom_call" | custom-call | tf_op jit(solution)/shard_map/pallas_call | solution.py:674
  134.5 1.7 %copy.10 = bf16[128,1024]{1,0:T(8,128)(2,1)} copy(bf16[128,1024]{1,0:T(8,128)(2,1)} %shard_map.82) | data formatting | bytes 524288
where the time goes:
time: 136 us
  Pallas kernels  134 us (99%)
  local copies, waits for them, and re-layouts  1.67 us (1%)
    pallas_call x1, Pallas kernels, block_call(): pl.pallas_call(functools.partial(block_kernel, devices), out_shape=jax.Sh...  134 us

commit v1 on v0

--- a/solution.py
+++ b/solution.py
@@ -67,31 +67,51 @@
 LANES = 128
 SLOT = 16
 COLS = 2
+CHUNKS = 4
 VMEM_BYTES = 66 * 1000 * 1000
 MESH = pl.DeviceIdType.MESH
 
 
+def choose(index, table):
+    value = jnp.int32(table[0])
+    for i in range(1, len(table)):
+        value = jnp.where(index == i, table[i], value)
+    return value
+
+
+def line_order(lines, nearest):
+    rows = []
+    for z in range(lines):
+        lower = z < lines - 1 - z
+        others = [line for line in range(lines) if line != z]
+        sign = 1 if nearest else -1
+        rows.append(sorted(others, key=lambda line: (sign * abs(line - z), (line > z) == lower)))
+    return [[rows[z][j] for z in range(lines)] for j in range(lines - 1)]
+
+
 def expert_kernel(
     devices, weight_copies,
-    normed, meta, state, modulation, gate_up, down,
+    normed, meta, state, modulation, wide,
     out,
-    tok, disp, gu, dn, hid_own, hid_other, got_meta, pick, slot_gate, got_x, got_up, got_down, acc,
-    meta_s, meta_r, ag_s, ag_r, core_r, hid_s, hid_r,
-    x_s, x_r, up_s, up_r, down_s, down_r,
+    tok, got_packed, got_rows, got_sum, disp, gu, dn, raised, hid_own, hid_other,
+    got_meta, pick, gated, squeeze, grow, acc,
+    meta_s, meta_r, z_s, z_r, x_s, x_r, core_s, core_r, hid_s, hid_r, rx_s, rx_r, rz_s, rz_r,
 ):
     me = lax.axis_index("dev")
     part = lax.axis_index("sub")
     other = 1 - part
     z = me // COLS
     x = me % COLS
-    across = z * COLS + (1 - x)
     lines = devices // COLS
     count, width = normed.shape
     half = width // 2
-    halves = gate_up.shape[0]
-    local = halves // 2
-    hidden = gate_up.shape[2]
+    local = raised.shape[0]
+    hidden = gu.shape[2]
+    both_hidden = 2 * hidden
     slots = local * SLOT
+    pack = local * CAP
+    rows = devices * SLOT
+    chunks, wide_chunk = tok.shape[1], tok.shape[3]
 
     def remote(src, dst, send, recv, where):
         return pltpu.make_async_remote_copy(
@@ -99,38 +119,66 @@
             device_id=where, device_id_type=MESH,
         )
 
-    def block(s, way, where, src=None):
-        dst = tok.at[part, s]
-        recv = core_r.at[s] if way == 3 else ag_r.at[s]
-        return remote(dst if src is None else src, dst, ag_s.at[s, way], recv, where)
-
-    up_to = {"dev": jnp.minimum(me + COLS, devices - 1)}
-    down_to = {"dev": jnp.maximum(me - COLS, 0)}
-    x_to = {"dev": across}
+    above = jnp.minimum(me + COLS, devices - 1)
+    below = jnp.maximum(me - COLS, 0)
+    x_to = {"dev": z * COLS + (1 - x)}
     core_to = {"sub": other}
     not_top = z < lines - 1
     not_bottom = z > 0
-    mine = normed.at[:, pl.ds(pl.multiple_of(part * half, LANES), half)]
-
-    def meta_copy(step):
-        target = (me + step) % devices
+    near_lines = [choose(z, table) for table in line_order(lines, True)]
+    far_lines = [choose(z, table) for table in line_order(lines, False)]
+
+    def lanes_of(c):
+        return pl.ds(pl.multiple_of(c * wide_chunk, wide_chunk), wide_chunk)
+
+    def own_lanes(c):
+        return pl.ds(pl.multiple_of(part * half + c * wide_chunk, wide_chunk), wide_chunk)
+
+    def slot_rows(s):
+        return pl.ds(pl.multiple_of(s * SLOT, SLOT), SLOT)
+
+    def meta_copy(line):
         return remote(
-            meta.at[pl.ds(pl.multiple_of(target * local, local), local)], got_meta.at[me],
-            meta_s.at[step - 1], meta_r.at[me], {"dev": target},
-        )
-
-    for step in range(1, devices):
-        meta_copy(step).start()
-
-    @pl.when(not_top)
-    def _():
-        block(me, 0, up_to, mine).start()
-
-    @pl.when(not_bottom)
-    def _():
-        block(me, 1, down_to, mine).start()
-
-    block(me, 2, x_to, mine).start()
+            meta.at[pl.ds(pl.multiple_of(line * COLS * local, COLS * local), COLS * local)],
+            got_meta.at[z], meta_s.at[line], meta_r.at[z], {"dev": line * COLS + x},
+        )
+
+    def meta_arrival(line):
+        return remote(got_meta.at[line], got_meta.at[line], meta_s.at[line], meta_r.at[line], x_to)
+
+    def z_copy(line, c, way, src=None):
+        dst = tok.at[line, c]
+        where = {"dev": jnp.where(way == 0, above, below)}
+        return remote(
+            dst if src is None else src, dst, z_s.at[line, c, way], z_r.at[line, c], where
+        )
+
+    def packed_out(line, c):
+        return wide.at[line, pl.ds(slots, pack), lanes_of(c)]
+
+    def x_copy(line, c):
+        return remote(
+            packed_out(line, c), got_packed.at[line, c], x_s.at[line, c], x_r.at[line, c], x_to
+        )
+
+    def core_copy(which, s, c):
+        place = disp.at[which, c, :, slot_rows(s), :]
+        return remote(place, place, core_s.at[s, c], core_r.at[s, c], core_to)
+
+    def own_send(c):
+        src = normed.at[:, own_lanes(c)]
+
+        @pl.when(not_top)
+        def _():
+            z_copy(z, c, 0, src).start()
+
+        @pl.when(not_bottom)
+        def _():
+            z_copy(z, c, 1, src).start()
+
+    own_send(0)
+    for line in near_lines:
+        meta_copy(line).start()
 
     before = (
         lax.broadcasted_iota(jnp.int32, (count, count), 0)
@@ -138,230 +186,282 @@
     ).astype(jnp.float32).astype(jnp.bfloat16)
     place = lax.broadcasted_iota(jnp.int32, (local, SLOT, count), 1).astype(jnp.float32)
 
-    def routing(s, gate):
-        chosen = jnp.where(gate > 0.0, 1.0, 0.0)
-        rank = jnp.dot(chosen.astype(jnp.bfloat16), before, preferred_element_type=jnp.float32)
-        rank = jnp.where(gate > 0.0, rank, -1.0)
-        hit = jnp.broadcast_to(rank[:, None, :], place.shape) == place
-        pick[s] = jnp.where(hit, 1.0, 0.0).reshape(slots, count).astype(jnp.bfloat16)
-        value = jnp.where(hit, jnp.broadcast_to(gate[:, None, :], place.shape), 0.0)
-        value = jnp.sum(value, -1, keepdims=True)
-        slot_gate[:, pl.ds(pl.multiple_of(s * SLOT, SLOT), SLOT), :] = jnp.broadcast_to(
-            value, (local, SLOT, LANES)
-        )
-
-    def dispatch(s, h, rows):
-        moved = jnp.dot(pick[s], rows, preferred_element_type=jnp.float32)
-        disp[h, :, pl.ds(pl.multiple_of(s * SLOT, SLOT), SLOT), :] = moved.astype(
-            jnp.bfloat16
-        ).reshape(local, SLOT, half)
-
-    routing(me, meta[pl.ds(pl.multiple_of(me * local, local), local)])
-    dispatch(me, 0, normed[:, :half])
-    dispatch(me, 1, normed[:, half:])
-    for step in range(1, devices):
-        s = (me + step) % devices
-        remote(
-            meta.at[pl.ds(0, local)], got_meta.at[s], meta_s.at[0], meta_r.at[s], {"dev": s}
-        ).wait_recv()
-        routing(s, got_meta[s])
-
-    def arrive(s):
-        block(s, 2, x_to).wait_recv()
-
-    def from_line(zz, way, where, more):
-        s = zz * COLS + x
-        arrive(s)
-
-        @pl.when(more)
-        def _():
-            block(s, way, where).start()
-
-        block(s, 2, x_to).start()
-        block(s, 3, core_to).start()
-        dispatch(s, part, tok[part, s])
-
-    def from_across(zz):
-        s = zz * COLS + (1 - x)
-        arrive(s)
-        block(s, 3, core_to).start()
-        dispatch(s, part, tok[part, s])
-
-    def from_core(s):
-        remote(tok.at[other, s], tok.at[other, s], ag_s.at[s, 3], core_r.at[s], core_to).wait_recv()
-        dispatch(s, other, tok[other, s])
-
-    def both(d, act):
-        @pl.when(z - d >= 0)
-        def _():
-            act(z - d, True)
-
-        @pl.when(z + d < lines)
-        def _():
-            act(z + d, False)
-
-    for d in range(1, lines):
-        both(d, lambda zz, low: from_line(
-            zz, 0 if low else 1, up_to if low else down_to, not_top if low else not_bottom
-        ))
-        if d == 1:
-            from_across(z)
-        else:
-            both(d - 1, lambda zz, low: from_core(zz * COLS + x))
-    both(lines - 1, lambda zz, low: from_core(zz * COLS + x))
-    from_core(across)
-    for d in range(1, lines):
-        both(d, lambda zz, low: from_across(zz))
-        if d > 1:
-            both(d - 1, lambda zz, low: from_core(zz * COLS + (1 - x)))
-    both(lines - 1, lambda zz, low: from_core(zz * COLS + (1 - x)))
-
-    @pl.when(not_top)
-    def _():
-        block(me, 0, up_to, mine).wait_send()
-
-    @pl.when(not_bottom)
-    def _():
-        block(me, 1, down_to, mine).wait_send()
-
-    block(me, 2, x_to, mine).wait_send()
-    for d in range(1, lines):
-
-        def sent(zz, low):
-            s = zz * COLS + x
-
-            @pl.when(not_top if low else not_bottom)
-            def _():
-                block(s, 0 if low else 1, up_to).wait_send()
-
-            block(s, 2, x_to).wait_send()
-            block(s, 3, core_to).wait_send()
-            block(zz * COLS + (1 - x), 3, core_to).wait_send()
-
-        both(d, sent)
-    block(across, 3, core_to).wait_send()
-
-    def hid_copy(h):
-        return remote(hid_own.at[h], hid_other.at[h], hid_s.at[h], hid_r.at[h], core_to)
+    def routing(line, ours, theirs):
+        for first, gate in ((True, ours), (False, theirs)):
+            chosen = jnp.where(gate > 0.0, 1.0, 0.0)
+            rank = jnp.dot(chosen.astype(jnp.bfloat16), before, preferred_element_type=jnp.float32)
+            rank = jnp.where(gate > 0.0, rank, -1.0)
+            hit = jnp.broadcast_to(rank[:, None, :], place.shape) == place
+            one = jnp.where(hit, 1.0, 0.0).reshape(slots, count).astype(jnp.bfloat16)
+            value = jnp.where(hit, jnp.broadcast_to(gate[:, None, :], place.shape), 0.0)
+            value = value.reshape(slots, count).astype(jnp.bfloat16)
+            if first:
+                pick[line, :slots] = one
+                gated[line, :slots] = value
+            else:
+                pick[line, slots:] = jnp.dot(
+                    squeeze[...], one, preferred_element_type=jnp.float32
+                ).astype(jnp.bfloat16)
+                gated[line, slots:] = jnp.dot(
+                    squeeze[...], value, preferred_element_type=jnp.float32
+                ).astype(jnp.bfloat16)
+
+    def expert_rows(base, column):
+        return pl.ds(pl.multiple_of(base + column * local, local), local)
+
+    def spread(line, c, block):
+        moved = jnp.dot(pick[line], block, preferred_element_type=jnp.float32).astype(jnp.bfloat16)
+        s = line * COLS + x
+        wide[line, slots:slots + pack, lanes_of(c)] = moved[slots:]
+        x_copy(line, c).start()
+        disp[part, c, :, slot_rows(s), :] = moved[:slots].reshape(local, SLOT, wide_chunk)
+        core_copy(part, s, c).start()
+
+    def own_step(c):
+        spread(z, c, normed[:, own_lanes(c)])
+
+    def line_step(line, c):
+        low = line < z
+
+        @pl.when(c == 0)
+        def _():
+            meta_arrival(line).wait_recv()
+            routing(
+                line, got_meta[line, expert_rows(0, x)], got_meta[line, expert_rows(0, 1 - x)]
+            )
+
+        way = jnp.where(low, 0, 1)
+        z_copy(line, c, way).wait_recv()
+
+        @pl.when(jnp.where(low, not_top, not_bottom))
+        def _():
+            z_copy(line, c, way).start()
+
+        spread(line, c, tok[line, c])
+
+    def x_step(line, c):
+        x_copy(line, c).wait_recv()
+        s = line * COLS + (1 - x)
+        disp[part, c, :, slot_rows(s), :] = jnp.dot(
+            grow[...], got_packed[line, c], preferred_element_type=jnp.float32
+        ).astype(jnp.bfloat16).reshape(local, SLOT, wide_chunk)
+        core_copy(part, s, c).start()
 
     def across_rows(left, right):
         return lax.dot_general(
             left, right, (((1,), (1,)), ((), ())), preferred_element_type=jnp.float32
         )
 
-    def raise_expert(e):
-        low, high = disp[0, e], disp[1, e]
-        for b in range(2):
-            h = 2 * e + b
-            weight_copies(h)[0].wait()
-
-            def product(g):
-                return across_rows(low, gu[h, g, :, :half]) + across_rows(high, gu[h, g, :, half:])
-
-            gate = product(0)
-            hid_own[h] = (gate * jax.nn.sigmoid(gate) * product(1)).astype(jnp.bfloat16)
-            hid_copy(h).start()
-
-    def lower_expert(e):
-        total = None
-        for b in range(2):
-            h = 2 * e + b
-            weight_copies(h)[1].wait()
-            hid_copy(h).wait_recv()
-            first = dn[h, pl.ds(pl.multiple_of(part * hidden, SLOT), hidden), :]
-            second = dn[h, pl.ds(pl.multiple_of(other * hidden, SLOT), hidden), :]
-            piece = jnp.dot(hid_own[h], first, preferred_element_type=jnp.float32) + jnp.dot(
-                hid_other[h], second, preferred_element_type=jnp.float32
+    def raise_part(e, c):
+        total = raised[e]
+        for side in range(2):
+            lanes = pl.ds(pl.multiple_of(side * half + c * wide_chunk, wide_chunk), wide_chunk)
+            weight = jnp.concatenate(
+                [gu[2 * e, 0, :, lanes], gu[2 * e + 1, 0, :, lanes],
+                 gu[2 * e, 1, :, lanes], gu[2 * e + 1, 1, :, lanes]], axis=0
             )
-            piece = piece.astype(jnp.bfloat16).astype(jnp.float32)
-            total = piece if total is None else total + piece
-        gain = slot_gate[e][:, :1]
-        disp[0, e] = (total * gain).astype(jnp.bfloat16)
-
-    raise_expert(0)
-
-    def step_expert(e, carry):
-        raise_expert(e)
-        lower_expert(e - 1)
+            total = total + across_rows(disp[side, c, e], weight)
+        return total
+
+    def hid_copy(e):
+        return remote(hid_own.at[e], hid_other.at[e], hid_s.at[e], hid_r.at[e], core_to)
+
+    def arrived(c):
+        for s in range(devices):
+            core_copy(other, s, c).wait_recv()
+
+    routing(
+        z, meta[expert_rows(z * COLS * local, x)], meta[expert_rows(z * COLS * local, 1 - x)]
+    )
+    own_step(0)
+
+    def weight_wait(h, carry):
+        for copy in weight_copies(h):
+            copy.wait()
         return carry
 
-    lax.fori_loop(1, local, step_expert, 0)
-    lower_expert(local - 1)
-
-    def combine(s):
-        rows = disp[0, :, pl.ds(pl.multiple_of(s * SLOT, SLOT), SLOT), :].reshape(slots, half)
-        return lax.dot_general(
-            pick[s], rows, (((0,), (0,)), ((), ())), preferred_element_type=jnp.float32
-        )
-
-    def x_copy(zz):
+    lax.fori_loop(0, 2 * local, weight_wait, 0)
+
+    def step(t, carry):
+        ready = t - lines
+
+        def raise_some(i):
+            first, last = i * local // (2 * lines), (i + 1) * local // (2 * lines)
+
+            @pl.when(ready >= 0)
+            def _():
+                if i == 0:
+                    arrived(ready)
+                for e in range(first, last):
+                    raised[e] = raise_part(e, ready)
+
+        @pl.when(t + 1 < chunks)
+        def _():
+            own_send(t + 1)
+            own_step(t + 1)
+
+        raise_some(0)
+        for j, line in enumerate(near_lines):
+            c = t - jnp.abs(line - z) + 1
+
+            @pl.when((c >= 0) & (c < chunks))
+            def _():
+                line_step(line, c)
+
+            raise_some(1 + j)
+
+        @pl.when(t < chunks)
+        def _():
+            x_step(z, t)
+
+        raise_some(lines)
+        for j, line in enumerate(near_lines):
+            c = t - jnp.abs(line - z)
+
+            @pl.when((c >= 0) & (c < chunks))
+            def _():
+                x_step(line, c)
+
+            raise_some(lines + 1 + j)
+        return carry
+
+    lax.fori_loop(0, chunks + lines - 1, step, 0)
+    arrived(chunks - 1)
+
+    def last_raise(e, carry):
+        total = raise_part(e, chunks - 1)
+        gate = total[:, :both_hidden]
+        hid_own[e] = (gate * jax.nn.sigmoid(gate) * total[:, both_hidden:]).astype(jnp.bfloat16)
+        hid_copy(e).start()
+        return carry
+
+    lax.fori_loop(0, local, last_raise, 0)
+
+    group = 2 * wide_chunk
+
+    def lower(g):
+        lanes = slice(g * group, (g + 1) * group)
+
+        def one(e, carry):
+            if g == 0:
+                hid_copy(e).wait_recv()
+            mine = pl.ds(pl.multiple_of(part * hidden, SLOT), hidden)
+            theirs = pl.ds(pl.multiple_of(other * hidden, SLOT), hidden)
+            left = jnp.concatenate([hid_own[e], hid_other[e]], axis=1)
+            right = jnp.concatenate(
+                [dn[2 * e, mine, lanes], dn[2 * e + 1, mine, lanes],
+                 dn[2 * e, theirs, lanes], dn[2 * e + 1, theirs, lanes]], axis=0
+            )
+            wide[e, :rows, lanes] = jnp.dot(
+                left, right, preferred_element_type=jnp.float32
+            ).astype(jnp.bfloat16)
+            return carry
+
+        lax.fori_loop(0, local, one, 0)
+
+    def result_rows(s, q):
+        return wide[:local, slot_rows(s), lanes_of(q)].reshape(slots, wide_chunk)
+
+    def rx_copy(line, q):
         return remote(
-            tok.at[0, zz * COLS + (1 - x)], got_x.at[zz], x_s.at[zz], x_r.at[zz], x_to
-        )
-
-    def line_copy(zz, low):
-        if low:
-            return remote(tok.at[1, zz], got_down.at[zz], down_s.at[zz], down_r.at[zz], down_to)
-        return remote(tok.at[1, zz], got_up.at[zz], up_s.at[zz], up_r.at[zz], up_to)
-
-    def give_across(zz, low):
-        s = zz * COLS + (1 - x)
-        tok[0, s] = combine(s).astype(jnp.bfloat16)
-        x_copy(zz).start()
-
-    def add_line(zz, low):
-        line_copy(zz, low).wait_recv()
-        acc[...] += (got_down if low else got_up)[zz].astype(jnp.float32)
-
-    def gather_here(zz):
-        acc[...] = combine(zz * COLS + x)
-        x_copy(zz).wait_recv()
-        acc[...] += got_x[zz].astype(jnp.float32)
-
-    def pass_on(zz, low):
-        gather_here(zz)
-
-        @pl.when(not_top if low else not_bottom)
-        def _():
-            add_line(zz, low)
-
-        tok[1, zz] = acc[...].astype(jnp.bfloat16)
-        line_copy(zz, low).start()
-
-    for d in range(lines - 1, 0, -1):
-        both(d, give_across)
-    give_across(z, False)
-    for d in range(lines - 1, 0, -1):
-        both(d, pass_on)
-    gather_here(z)
-
-    @pl.when(not_bottom)
-    def _():
-        add_line(z, False)
-
-    @pl.when(not_top)
-    def _():
-        add_line(z, True)
-
-    own = pl.ds(pl.multiple_of(part * half, LANES), half)
-    out[...] = (state[:, own] + (1.0 + modulation[3:4, own]) * acc[...]).astype(out.dtype)
-
-    for d in range(1, lines):
-
-        def drained(zz, low):
-            line_copy(zz, low).wait_send()
-            x_copy(zz).wait_send()
-
-        both(d, drained)
-    x_copy(z).wait_send()
-    for step in range(1, devices):
-        meta_copy(step).wait_send()
-
-    def hid_drain(h, carry):
-        hid_copy(h).wait_send()
+            wide.at[lines + line, pl.ds(slots, pack), lanes_of(q)], got_rows.at[line, q],
+            rx_s.at[line, q], rx_r.at[line, q], x_to,
+        )
+
+    def rz_copy(line, q, way):
+        where = {"dev": jnp.where(way == 0, above, below)}
+        return remote(
+            tok.at[line, q], got_sum.at[way, line, q],
+            rz_s.at[line, q], rz_r.at[way, line, q], where,
+        )
+
+    def give(line, q):
+        packed = jnp.dot(
+            squeeze[...], result_rows(line * COLS + (1 - x), q), preferred_element_type=jnp.float32
+        )
+        wide[lines + line, slots:slots + pack, lanes_of(q)] = packed.astype(jnp.bfloat16)
+        rx_copy(line, q).start()
+
+    def gather_here(line, q):
+        rx_copy(line, q).wait_recv()
+        pieces = jnp.concatenate([result_rows(line * COLS + x, q), got_rows[line, q]], axis=0)
+        acc[...] = lax.dot_general(
+            gated[line], pieces, (((0,), (0,)), ((), ())), preferred_element_type=jnp.float32
+        )
+
+    def add_line(line, q, way):
+        rz_copy(line, q, way).wait_recv()
+        acc[...] += got_sum[way, line, q].astype(jnp.float32)
+
+    def pass_on(line, q):
+        gather_here(line, q)
+        way = jnp.where(line > z, 0, 1)
+
+        @pl.when(jnp.where(line > z, not_bottom, not_top))
+        def _():
+            add_line(line, q, way)
+
+        tok[line, q] = acc[...].astype(jnp.bfloat16)
+        rz_copy(line, q, way).start()
+
+    for g in range(half // group):
+        lower(g)
+        for q in range(2 * g, 2 * g + 2):
+            give(far_lines[0], q)
+    for line in far_lines[1:] + [z]:
+        lax.fori_loop(0, chunks, lambda q, carry, line=line: (give(line, q), carry)[1], 0)
+    for line in near_lines:
+        low = line < z
+
+        @pl.when(jnp.where(low, not_top, not_bottom))
+        def _():
+            for c in range(chunks):
+                z_copy(line, c, jnp.where(low, 0, 1)).wait_send()
+
+    for line in far_lines:
+        lax.fori_loop(0, chunks, lambda q, carry, line=line: (pass_on(line, q), carry)[1], 0)
+    for q in range(chunks):
+        gather_here(z, q)
+
+        @pl.when(not_bottom)
+        def _():
+            add_line(z, q, 0)
+
+        @pl.when(not_top)
+        def _():
+            add_line(z, q, 1)
+
+        own = own_lanes(q)
+        lanes = slice(q * wide_chunk, (q + 1) * wide_chunk)
+        out[:, lanes] = (
+            state[:, own] + (1.0 + modulation[3:4, own]) * acc[...]
+        ).astype(out.dtype)
+
+    for c in range(chunks):
+
+        @pl.when(not_top)
+        def _():
+            z_copy(z, c, 0, normed.at[:, own_lanes(c)]).wait_send()
+
+        @pl.when(not_bottom)
+        def _():
+            z_copy(z, c, 1, normed.at[:, own_lanes(c)]).wait_send()
+
+        for line in near_lines:
+            rz_copy(line, c, jnp.where(line > z, 0, 1)).wait_send()
+        for line in range(lines):
+            x_copy(line, c).wait_send()
+            rx_copy(line, c).wait_send()
+        for s in range(devices):
+            core_copy(part, s, c).wait_send()
+    for line in near_lines:
+        meta_copy(line).wait_send()
+
+    def hid_drain(e, carry):
+        hid_copy(e).wait_send()
         return carry
 
-    lax.fori_loop(0, halves, hid_drain, 0)
+    lax.fori_loop(0, local, hid_drain, 0)
 
 
 def front_kernel(
@@ -621,10 +721,11 @@
 def block_kernel(devices, *refs):
     sources, gate_up, down, out = refs[:6], refs[6], refs[7], refs[8]
     held, normed, state, meta = refs[9:15], refs[15], refs[16], refs[17]
-    front_buffers, expert_buffers = refs[18:23], refs[23:36]
-    own_sem, gu_sem, dn_sem = refs[36:39]
-    front_sems, expert_sems = refs[39:48], refs[48:]
-    gu, dn = expert_buffers[2:4]
+    front_buffers, expert_buffers = refs[18:23], refs[23:39]
+    own_sem, gu_sem, dn_sem = refs[39:42]
+    front_sems, expert_sems = refs[42:51], refs[51:]
+    gu, dn, raised = expert_buffers[5:8]
+    squeeze, grow = expert_buffers[13:15]
     halves = gate_up.shape[0]
 
     def weight_copies(h):
@@ -640,13 +741,20 @@
             return carry
 
         lax.fori_loop(0, halves, one, 0)
+        raised[...] = jnp.zeros_like(raised)
+        for ref, axis in ((squeeze, 0), (grow, 1)):
+            packed = lax.broadcasted_iota(jnp.int32, ref.shape, axis)
+            slot = lax.broadcasted_iota(jnp.int32, ref.shape, 1 - axis)
+            inner = slot & (SLOT - 1)
+            same = (packed == (slot - inner) // SLOT * CAP + inner) & (inner < CAP)
+            ref[...] = jnp.where(same, 1.0, 0.0).astype(jnp.bfloat16)
 
     front_kernel(
         devices, start_weights, sources, held, own_sem, normed, state, meta,
         *front_buffers, *front_sems,
     )
     expert_kernel(
-        devices, weight_copies, normed, meta, state, held[3], gate_up, down, out,
+        devices, weight_copies, normed, meta, state, held[3], front_buffers[1], out,
         *expert_buffers, *expert_sems,
     )
 
@@ -664,6 +772,8 @@
     hidden = gate_up_weight.shape[2]
     lines = devices // COLS
     rows = devices * SLOT
+    slots, pack = local * SLOT, local * CAP
+    part = half // CHUNKS
     shard = out_weight.shape[0]
     own = (
         tokens, query_key_value.transpose(1, 0, 2), out_weight, modulation,
@@ -686,26 +796,33 @@
             pltpu.VMEM((count, half), jnp.bfloat16),
             pltpu.VMEM((devices, count, shard), jnp.float32),
             pltpu.VMEM((devices, count, shard), jnp.float32),
-            pltpu.VMEM((2, devices, count, half), jnp.bfloat16),
-            pltpu.VMEM((2, local, rows, half), jnp.bfloat16),
+            pltpu.VMEM((lines, CHUNKS, count, part), jnp.bfloat16),
+            pltpu.VMEM((lines, CHUNKS, pack, part), jnp.bfloat16),
+            pltpu.VMEM((lines, CHUNKS, pack, part), jnp.bfloat16),
+            pltpu.VMEM((2, lines, CHUNKS, count, part), jnp.bfloat16),
+            pltpu.VMEM((2, CHUNKS, local, rows, part), jnp.bfloat16),
             pltpu.VMEM(gate_up_weight.shape, jnp.bfloat16),
             pltpu.VMEM(down_weight.shape, jnp.bfloat16),
-            pltpu.VMEM((halves, rows, hidden), jnp.bfloat16),
-            pltpu.VMEM((halves, rows, hidden), jnp.bfloat16),
-            pltpu.VMEM((devices, local, count), jnp.float32),
-            pltpu.VMEM((devices, local * SLOT, count), jnp.bfloat16),
-            pltpu.VMEM((local, rows, LANES), jnp.float32),
-            pltpu.VMEM((lines, count, half), jnp.bfloat16),
-            pltpu.VMEM((lines, count, half), jnp.bfloat16),
-            pltpu.VMEM((lines, count, half), jnp.bfloat16),
-            pltpu.VMEM((count, half), jnp.float32),
+            pltpu.VMEM((local, rows, 4 * hidden), jnp.float32),
+            pltpu.VMEM((local, rows, 2 * hidden), jnp.bfloat16),
+            pltpu.VMEM((local, rows, 2 * hidden), jnp.bfloat16),
+            pltpu.VMEM((lines, COLS * local, count), jnp.float32),
+            pltpu.VMEM((lines, slots + pack, count), jnp.bfloat16),
+            pltpu.VMEM((lines, slots + pack, count), jnp.bfloat16),
+            pltpu.VMEM((pack, slots), jnp.bfloat16),
+            pltpu.VMEM((slots, pack), jnp.bfloat16),
+            pltpu.VMEM((count, part), jnp.float32),
             dma((6,)), dma((halves,)), dma((halves,)),
             dma((2,)), dma((2,)), dma((2,)), dma((2,)),
             dma((devices, 4)), dma((devices,)), dma((devices,)),
             dma((devices,)), dma((devices,)),
-            dma((devices,)), dma((devices,)), dma((devices, 4)), dma((devices,)), dma((devices,)),
-            dma((halves,)), dma((halves,)),
-            dma((lines,)), dma((lines,)), dma((lines,)), dma((lines,)), dma((lines,)), dma((lines,)),
+            dma((lines,)), dma((lines,)),
+            dma((lines, CHUNKS, 2)), dma((lines, CHUNKS)),
+            dma((lines, CHUNKS)), dma((lines, CHUNKS)),
+            dma((devices, CHUNKS)), dma((devices, CHUNKS)),
+            dma((local,)), dma((local,)),
+            dma((lines, CHUNKS)), dma((lines, CHUNKS)),
+            dma((lines, CHUNKS)), dma((2, lines, CHUNKS)),
         ],
         compiler_params=pltpu.CompilerParams(
             collective_id=1, has_side_effects=True, vmem_limit_bytes=VMEM_BYTES
@@ -735,7 +852,11 @@
     token_bytes = 12 * devices * count * width
     fits = weight_bytes + token_bytes < VMEM_BYTES and CAP <= SLOT
     paired = parts == 2 and lax.axis_size("groups") == 2 and devices % COLS == 0
+    experts_here = gate_up_weight.shape[0] // 2
     tiled = out_weight.shape[0] % (2 * LANES) == 0 and count == LANES
+    tiled = tiled and down_weight.shape[2] % (2 * CHUNKS * LANES) == 0 and experts_here == devices
+    tiled = tiled and experts_here * (SLOT + CAP) <= out_weight.shape[0] and SLOT * devices == LANES
+    tiled = tiled and gate_up_weight.shape[3] % 64 == 0
     if fits and paired and tiled:
         return block_call(
             tokens, query_key_value, out_weight, modulation, router_weight, expert_ids,

time: 136 us -> 123 us (0.904); the launches traced: 136 us -> 122 us
  Pallas kernels: 134 us -> 120 us
    pallas_call x1, Pallas kernels: 134 us -> 120 us  [block_call(): pl.pallas_call(functools.partial(block_kernel, devices), out_shape=jax.Sh...]
where the time goes in v1:
time: 123 us; the launch traced here: 122 us
  Pallas kernels  120 us (98%)
  local copies, waits for them, and re-layouts  1.67 us (1%)
    pallas_call x1, Pallas kernels, block_call(): pl.pallas_call(functools.partial(block_kernel, devices), out_shape=jax.Sh...  120 us

profile of v1, /device:TPU:0, one launch (start us, length us, event | category | flops | bytes accessed | tf_op | source)
XLA Modules:
  0.0 121.6 jit_solution(9646359104856249438)
XLA Ops:
  0.0 119.9 %shard_map.82 = bf16[128,1024]{1,0:T(8,128)(2,1)} custom-call(bf16[128,2048]{1,0:T(8,128)(2,1)} %refs_0_.1, bf16[3,128,1024]{2,1,0:T(8,128)(2,1)} %bitcast.5, bf16[256,1024]{1,0:T(8,128)(2,1)} %refs_2_.1, f32[4,2048]{1,0:T(4,128)} %refs_3_.1, bf16[64,2048]{1,0:T(8,128)(2,1)} %bitcast.6, s32[4,128]{1,0:T(4,128)} %bitcast.7, ...), custom_call_target="tpu_custom_call" | custom-call | tf_op jit(solution)/shard_map/pallas_call | solution.py:784
  119.9 1.7 %copy.10 = bf16[128,1024]{1,0:T(8,128)(2,1)} copy(bf16[128,1024]{1,0:T(8,128)(2,1)} %shard_map.82) | data formatting | bytes 524288

commit v2 on v1

--- a/solution.py
+++ b/solution.py
@@ -68,6 +68,7 @@
 SLOT = 16
 COLS = 2
 CHUNKS = 4
+PIECES = 2
 VMEM_BYTES = 66 * 1000 * 1000
 MESH = pl.DeviceIdType.MESH
 
@@ -468,44 +469,49 @@
     devices, start_weights,
     sources, held, own_sem,
     normed, state, meta,
-    near, wide, mixed, mine_out, their_out,
-    near_s, near_r, far_s, far_r, ag_s, ag_r, y_r, sum_s, sum_r,
+    near, column, mixed, mixed_in, mine_out, their_out, sent_back, got_back, their_back,
+    near_s, near_r, far_s, far_r, wz_s, wz_r, wy_s, wy_r, mix_s, mix_r,
+    sum_s, sum_r, back_s, back_r, share_s, share_r,
 ):
     packed_hbm, weight_hbm = sources[1], sources[2]
-    tokens, packed, weight, modulation, router, ids = held
-
-    def own_copy(i):
-        return pltpu.make_async_copy(sources[i], held[i], own_sem.at[i])
-
-    for i in (1, 2, 0, 3, 4, 5):
-        own_copy(i).start()
+    tokens, packed, modulation, router, ids = held
     me = lax.axis_index("dev")
     part = lax.axis_index("sub")
     group = lax.axis_index("groups")
     z = me // COLS
     x = me % COLS
-    across = z * COLS + (1 - x)
     lines = devices // COLS
     count, width = tokens.shape
-    shard = weight.shape[0]
-    extra = shard * 3 // 8 // SLOT * SLOT
-    main = shard - extra
+    shard = column.shape[1]
+    share = shard // 2
+    piece = share // PIECES
+    pairs, pair = near.shape[1], near.shape[4]
+    targets = (tokens, packed, column.at[z], modulation, router, ids)
+
+    def own_copy(i):
+        return pltpu.make_async_copy(sources[i], targets[i], own_sem.at[i])
+
+    for i in (1, 2, 0, 3, 4, 5):
+        own_copy(i).start()
     not_top = z < lines - 1
     not_bottom = z > 0
-    up_to = {"dev": jnp.minimum(me + COLS, devices - 1)}
-    down_to = {"dev": jnp.maximum(me - COLS, 0)}
-    x_to = {"dev": across}
+    above = jnp.minimum(me + COLS, devices - 1)
+    below = jnp.maximum(me - COLS, 0)
+    x_to = {"dev": z * COLS + (1 - x)}
     y_to = {"groups": 1 - group}
     core_to = {"sub": 1 - part}
+    near_lines = [choose(z, table) for table in line_order(lines, True)]
 
     barrier = pltpu.get_barrier_semaphore()
-    for step in range(1, devices):
-        pl.semaphore_signal(
-            barrier, inc=1, device_id={"dev": (me + step) % devices}, device_id_type=MESH
-        )
-    pl.semaphore_signal(barrier, inc=1, device_id=core_to, device_id_type=MESH)
-    pl.semaphore_signal(barrier, inc=1, device_id=y_to, device_id_type=MESH)
-    pl.semaphore_wait(barrier, devices + 1)
+
+    def greet(where):
+        pl.semaphore_signal(barrier, inc=1, device_id=where, device_id_type=MESH)
+
+    for where in (x_to, y_to, core_to):
+        greet(where)
+    for line in near_lines:
+        greet({"dev": line * COLS + x})
+    pl.semaphore_wait(barrier, lines + 2)
 
     def remote(src, dst, send, recv, where):
         return pltpu.make_async_remote_copy(
@@ -513,160 +519,233 @@
             device_id=where, device_id_type=MESH,
         )
 
-    def near_copy(i):
-        return remote(packed_hbm.at[1 + i], near.at[x, i], near_s.at[i], near_r.at[i], x_to)
-
-    def far_copy(i, where):
-        return remote(near.at[1 - x, i], near.at[x, i], far_s.at[i], far_r.at[i], where)
-
-    def piece(s, way, where, src=None):
-        start, size = (main, extra) if way == 3 else (extra, main)
-        dst = wide.at[s, pl.ds(pl.multiple_of(group * start, SLOT), size)]
-        recv = y_r.at[s] if way == 3 else ag_r.at[s]
-        return remote(dst if src is None else src, dst, ag_s.at[s, way], recv, where)
-
-    far_up = (x == 0) & not_top
-    far_down = (x == 1) & not_bottom
+    def near_copy(k):
+        src = packed_hbm.at[1:3, :, pl.ds(k * pair, pair)]
+        return remote(src, near.at[x, k], near_s.at[k], near_r.at[k], x_to)
+
+    def far_copy(k):
+        where = {"dev": jnp.where(x == 0, above, below)}
+        return remote(near.at[1 - x, k], near.at[x, k], far_s.at[k], far_r.at[k], where)
+
+    give_far = ((x == 0) & not_top) | ((x == 1) & not_bottom)
     have_far = ((x == 0) & not_bottom) | ((x == 1) & not_top)
-    mine = weight_hbm.at[pl.ds(pl.multiple_of(group * extra, SLOT), main)]
-
-    for i in range(2):
-        near_copy(i).start()
-
-    @pl.when(not_top)
-    def _():
-        piece(me, 0, up_to, mine).start()
-
-    @pl.when(not_bottom)
-    def _():
-        piece(me, 1, down_to, mine).start()
-
-    piece(me, 2, x_to, mine).start()
+
+    def piece_rows(which, i):
+        return pl.ds(pl.multiple_of(which * share + i * piece, SLOT), piece)
+
+    def wz_copy(line, i, way, src=None):
+        dst = column.at[line, piece_rows(group, i)]
+        where = {"dev": jnp.where(way == 0, above, below)}
+        return remote(
+            dst if src is None else src, dst, wz_s.at[line, i, way], wz_r.at[line, i], where
+        )
+
+    def own_piece(i):
+        return weight_hbm.at[piece_rows(group, i)]
+
+    def wy_copy(line, i, which):
+        block = column.at[line, piece_rows(which, i)]
+        return remote(block, block, wy_s.at[line, i], wy_r.at[line, i], y_to)
+
+    for k in range(pairs):
+        near_copy(k).start()
+    for i in range(PIECES):
+
+        @pl.when(not_top)
+        def _():
+            wz_copy(z, i, 0, own_piece(i)).start()
+
+        @pl.when(not_bottom)
+        def _():
+            wz_copy(z, i, 1, own_piece(i)).start()
+
     start_weights()
 
     @pl.when(jnp.logical_not(have_far))
     def _():
         near[x] = jnp.zeros_like(near[x])
 
-    for i in range(2):
-        near_copy(i).wait_recv()
-
-        @pl.when(far_up)
-        def _():
-            far_copy(i, up_to).start()
-
-        @pl.when(far_down)
-        def _():
-            far_copy(i, down_to).start()
-
-    def both(d, act):
-        @pl.when(z - d >= 0)
-        def _():
-            act(z - d, True)
-
-        @pl.when(z + d < lines)
-        def _():
-            act(z + d, False)
-
-    def project(s, block):
-        mine_out[s] = lax.dot_general(
-            mixed[...], block, (((1,), (1,)), ((), ())), preferred_element_type=jnp.float32
-        )
-        sum_copy(s).start()
-
-    def sum_copy(s):
-        return remote(mine_out.at[s], their_out.at[s], sum_s.at[s], sum_r.at[s], core_to)
-
-    def take_line(zz, low):
-        s = zz * COLS + x
-        piece(s, 2, x_to).wait_recv()
-
-        @pl.when(not_top if low else not_bottom)
-        def _():
-            piece(s, 0 if low else 1, up_to if low else down_to).start()
-
-        piece(s, 2, x_to).start()
-        piece(s, 3, y_to).start()
-
-    def take_across(zz, low):
-        s = zz * COLS + (1 - x)
-        piece(s, 2, x_to).wait_recv()
-        piece(s, 3, y_to).start()
-
-    def take_y(s):
-        dst = wide.at[s, pl.ds(pl.multiple_of((1 - group) * main, SLOT), extra)]
-        remote(dst, dst, ag_s.at[s, 3], y_r.at[s], y_to).wait_recv()
-        project(s, wide[s])
-
-    def line_y(zz, low):
-        take_y(zz * COLS + x)
-
-    def across_y(zz, low):
-        take_y(zz * COLS + (1 - x))
-
-    both(1, take_line)
-    take_across(z, False)
-    for d in range(2, min(3, lines)):
-        both(d, take_line)
+    def way_of(line):
+        return jnp.where(line < z, 0, 1)
+
+    def more(line):
+        return jnp.where(line < z, not_top, not_bottom)
+
+    def busy(line):
+        return jnp.where(line < z, x == 0, x == 1)
+
+    def distance(line):
+        return jnp.abs(line - z)
+
+    def take(line, onward):
+        for i in range(PIECES):
+            wz_copy(line, i, way_of(line)).wait_recv()
+
+            @pl.when(onward)
+            def _():
+                wz_copy(line, i, way_of(line)).start()
+
+            wy_copy(line, i, group).start()
+
+    def pass_near(k):
+        near_copy(k).wait_recv()
+
+        @pl.when(give_far)
+        def _():
+            far_copy(k).start()
+
+    early = pairs // 2
+    for k in range(early):
+        pass_near(k)
+    for line in near_lines:
+
+        @pl.when(distance(line) == 1)
+        def _():
+            take(line, more(line) & jnp.logical_not(busy(line)))
+
+    for k in range(early, pairs):
+        pass_near(k)
+    for line in near_lines:
+
+        @pl.when((distance(line) == 1) & busy(line) & more(line))
+        def _():
+            for i in range(PIECES):
+                wz_copy(line, i, way_of(line)).start()
+
     for i in range(6):
         own_copy(i).wait()
-
-    @pl.when(have_far)
-    def _():
-        for i in range(2):
-            far_copy(i, x_to).wait_recv()
 
     row = lax.broadcasted_iota(jnp.int32, (count, count), 0)
     col = lax.broadcasted_iota(jnp.int32, (count, count), 1)
     see_before = (col >= row) & (me > 0)
     see_after = (col <= row) & (me < devices - 1)
-    for h in range(mixed.shape[1] // HEAD):
-        lanes = slice(h * HEAD, (h + 1) * HEAD)
-        query = packed[0, :, lanes]
-
-        def score(keys):
-            return lax.dot_general(
-                query, keys, (((1,), (1,)), ((), ())), preferred_element_type=jnp.float32
-            ) / math.sqrt(HEAD)
-
-        scores = jnp.concatenate(
-            [
-                jnp.where(see_before, score(near[0, 0, :, lanes]), NEG),
-                score(packed[1, :, lanes]),
-                jnp.where(see_after, score(near[1, 0, :, lanes]), NEG),
-            ],
-            axis=1,
-        )
-        top = jnp.max(scores, -1, keepdims=True)
-        share = jnp.exp(scores - top)
-        share = (share / jnp.sum(share, -1, keepdims=True)).astype(jnp.bfloat16)
-        values = jnp.concatenate(
-            [near[0, 1, :, lanes], packed[2, :, lanes], near[1, 1, :, lanes]], axis=0
-        )
-        mixed[:, lanes] = jnp.dot(
-            share, values, preferred_element_type=jnp.float32
-        ).astype(jnp.bfloat16)
-
-    project(me, weight[...])
-    for d in range(3, lines):
-        both(d, take_line)
-    for d in range(1, lines):
-        both(d, line_y)
-        both(d, take_across)
-        if d == 1:
-            take_y(across)
-    for d in range(1, lines):
-        both(d, across_y)
+
+    def mix_copy(k):
+        lanes = pl.ds(k * pair, pair)
+        return remote(
+            mixed.at[:, lanes], mixed_in.at[:, lanes], mix_s.at[k], mix_r.at[k], x_to
+        )
+
+    for k in range(pairs):
+
+        @pl.when(have_far)
+        def _():
+            far_copy(k).wait_recv()
+
+        for h in range(pair // HEAD):
+            lanes = slice(k * pair + h * HEAD, k * pair + (h + 1) * HEAD)
+            inner = slice(h * HEAD, (h + 1) * HEAD)
+            query = packed[0, :, lanes]
+
+            def score(keys):
+                return lax.dot_general(
+                    query, keys, (((1,), (1,)), ((), ())), preferred_element_type=jnp.float32
+                ) / math.sqrt(HEAD)
+
+            scores = jnp.concatenate(
+                [
+                    jnp.where(see_before, score(near[0, k, 0, :, inner]), NEG),
+                    score(packed[1, :, lanes]),
+                    jnp.where(see_after, score(near[1, k, 0, :, inner]), NEG),
+                ],
+                axis=1,
+            )
+            top = jnp.max(scores, -1, keepdims=True)
+            weight = jnp.exp(scores - top)
+            weight = (weight / jnp.sum(weight, -1, keepdims=True)).astype(jnp.bfloat16)
+            values = jnp.concatenate(
+                [near[0, k, 1, :, inner], packed[2, :, lanes], near[1, k, 1, :, inner]], axis=0
+            )
+            mixed[:, lanes] = jnp.dot(
+                weight, values, preferred_element_type=jnp.float32
+            ).astype(jnp.bfloat16)
+        mix_copy(k).start()
+        if k + 1 == early:
+            for line in near_lines:
+
+                @pl.when((distance(line) == 2) & jnp.logical_not(busy(line)))
+                def _():
+                    take(line, more(line))
+
+    for k in range(pairs):
+        mix_copy(k).wait_recv()
+
+    def place_of(which):
+        return group if which == 0 else 1 - group
+
+    def sum_copy(line, which):
+        place = place_of(which)
+        return remote(
+            mine_out.at[line, place], their_out.at[line, place],
+            sum_s.at[line, which], sum_r.at[line, which], core_to,
+        )
+
+    def back_copy(line, which):
+        place = place_of(which)
+        return remote(
+            sent_back.at[line, place], got_back.at[line, place],
+            back_s.at[line, which], back_r.at[line, which], x_to,
+        )
+
+    def share_copy(line, which):
+        place = place_of(which)
+        return remote(
+            got_back.at[line, place], their_back.at[line, place],
+            share_s.at[line, which], share_r.at[line, which], core_to,
+        )
+
+    def project(line, which):
+        place = place_of(which)
+        block = column[line, pl.ds(pl.multiple_of(place * share, SLOT), share), :]
+        both = jnp.concatenate([mixed_in[...], mixed[...]], axis=0)
+        product = lax.dot_general(
+            both, block, (((1,), (1,)), ((), ())), preferred_element_type=jnp.float32
+        )
+        sent_back[line, place] = product[:count].astype(jnp.bfloat16)
+        back_copy(line, which).start()
+        mine_out[line, place] = product[count:]
+        sum_copy(line, which).start()
+
+    steps = [(line, which) for line in [z] + near_lines for which in range(2)]
+
+    def relay(i):
+        back_copy(*steps[i]).wait_recv()
+        share_copy(*steps[i]).start()
+
+    for i, (line, which) in enumerate(steps):
+        if i >= 2:
+            if which == 0:
+
+                @pl.when((distance(line) > 2) | ((distance(line) == 2) & busy(line)))
+                def _():
+                    take(line, more(line))
+            else:
+                for n in range(PIECES):
+                    wy_copy(line, n, 1 - group).wait_recv()
+        project(line, which)
+        if i >= 2:
+            relay(i - 2)
+    relay(len(steps) - 2)
+    relay(len(steps) - 1)
 
     square = jnp.zeros((count, 1), jnp.float32)
-    for s in range(devices):
-        sum_copy(s).wait_recv()
-        lanes = slice(s * shard, (s + 1) * shard)
-        value = tokens[:, lanes].astype(jnp.float32) + (1.0 + modulation[0:1, lanes]) * (
-            mine_out[s] + their_out[s]
-        )
-        state[:, lanes] = value
-        square = square + jnp.sum(value * value, -1, keepdims=True)
+    for line, which in steps:
+        place = place_of(which)
+        sum_copy(line, which).wait_recv()
+        share_copy(line, which).wait_recv()
+        for column_of, total in (
+            (x, mine_out[line, place] + their_out[line, place]),
+            (
+                1 - x,
+                got_back[line, place].astype(jnp.float32)
+                + their_back[line, place].astype(jnp.float32),
+            ),
+        ):
+            start = (line * COLS + column_of) * shard + place * share
+            lanes = pl.ds(pl.multiple_of(start, LANES), share)
+            value = tokens[:, lanes].astype(jnp.float32) + (1.0 + modulation[0:1, lanes]) * total
+            state[:, lanes] = value
+            square = square + jnp.sum(value * value, -1, keepdims=True)
     scale = lax.rsqrt(square / width + EPS)
     for s in range(devices):
         lanes = slice(s * shard, (s + 1) * shard)
@@ -683,47 +762,43 @@
     lifted = jnp.where(named, jax.nn.sigmoid(logits), 0.0)
     meta[...] = lifted / jnp.sum(lifted, 0, keepdims=True)
 
-    for i in range(2):
-        near_copy(i).wait_send()
-
-        @pl.when(far_up | far_down)
-        def _():
-            far_copy(i, x_to).wait_send()
-
-    @pl.when(not_top)
-    def _():
-        piece(me, 0, up_to, mine).wait_send()
-
-    @pl.when(not_bottom)
-    def _():
-        piece(me, 1, down_to, mine).wait_send()
-
-    piece(me, 2, x_to, mine).wait_send()
-    piece(across, 3, y_to).wait_send()
-    for d in range(1, lines):
-
-        def sent(zz, low):
-            s = zz * COLS + x
-
-            @pl.when(not_top if low else not_bottom)
+    for k in range(pairs):
+        near_copy(k).wait_send()
+        mix_copy(k).wait_send()
+
+        @pl.when(give_far)
+        def _():
+            far_copy(k).wait_send()
+
+    for i in range(PIECES):
+
+        @pl.when(not_top)
+        def _():
+            wz_copy(z, i, 0, own_piece(i)).wait_send()
+
+        @pl.when(not_bottom)
+        def _():
+            wz_copy(z, i, 1, own_piece(i)).wait_send()
+
+        for line in near_lines:
+
+            @pl.when(more(line))
             def _():
-                piece(s, 0 if low else 1, up_to).wait_send()
-
-            piece(s, 2, x_to).wait_send()
-            piece(s, 3, y_to).wait_send()
-            piece(zz * COLS + (1 - x), 3, y_to).wait_send()
-
-        both(d, sent)
-    for s in range(devices):
-        sum_copy(s).wait_send()
+                wz_copy(line, i, way_of(line)).wait_send()
+
+            wy_copy(line, i, group).wait_send()
+    for line, which in steps:
+        sum_copy(line, which).wait_send()
+        back_copy(line, which).wait_send()
+        share_copy(line, which).wait_send()
 
 
 def block_kernel(devices, *refs):
     sources, gate_up, down, out = refs[:6], refs[6], refs[7], refs[8]
-    held, normed, state, meta = refs[9:15], refs[15], refs[16], refs[17]
-    front_buffers, expert_buffers = refs[18:23], refs[23:39]
-    own_sem, gu_sem, dn_sem = refs[39:42]
-    front_sems, expert_sems = refs[42:51], refs[51:]
+    held, normed, state, meta, wide = refs[9:14], refs[14], refs[15], refs[16], refs[17]
+    front_buffers, expert_buffers = refs[18:27], refs[27:43]
+    own_sem, gu_sem, dn_sem = refs[43:46]
+    front_sems, expert_sems = refs[46:62], refs[62:]
     gu, dn, raised = expert_buffers[5:8]
     squeeze, grow = expert_buffers[13:15]
     halves = gate_up.shape[0]
@@ -754,7 +829,7 @@
         *front_buffers, *front_sems,
     )
     expert_kernel(
-        devices, weight_copies, normed, meta, state, held[3], front_buffers[1], out,
+        devices, weight_copies, normed, meta, state, held[2], wide, out,
         *expert_buffers, *expert_sems,
     )
 
@@ -787,15 +862,20 @@
         in_specs=[hbm] * 8,
         out_specs=pl.BlockSpec(memory_space=pltpu.VMEM),
         scratch_shapes=[
-            *[pltpu.VMEM(array.shape, array.dtype) for array in own],
+            *[pltpu.VMEM(own[i].shape, own[i].dtype) for i in (0, 1, 3, 4, 5)],
             pltpu.VMEM((count, width), jnp.bfloat16),
             pltpu.VMEM((count, width), jnp.float32),
             pltpu.VMEM((router_weight.shape[1], count), jnp.float32),
-            pltpu.VMEM((2, 2, count, half), jnp.bfloat16),
-            pltpu.VMEM((devices, shard, half), jnp.bfloat16),
+            pltpu.VMEM((devices, slots + pack, half), jnp.bfloat16),
+            pltpu.VMEM((2, CHUNKS, 2, count, part), jnp.bfloat16),
+            pltpu.VMEM((lines, shard, half), jnp.bfloat16),
             pltpu.VMEM((count, half), jnp.bfloat16),
-            pltpu.VMEM((devices, count, shard), jnp.float32),
-            pltpu.VMEM((devices, count, shard), jnp.float32),
+            pltpu.VMEM((count, half), jnp.bfloat16),
+            pltpu.VMEM((lines, 2, count, shard // 2), jnp.float32),
+            pltpu.VMEM((lines, 2, count, shard // 2), jnp.float32),
+            pltpu.VMEM((lines, 2, count, shard // 2), jnp.bfloat16),
+            pltpu.VMEM((lines, 2, count, shard // 2), jnp.bfloat16),
+            pltpu.VMEM((lines, 2, count, shard // 2), jnp.bfloat16),
             pltpu.VMEM((lines, CHUNKS, count, part), jnp.bfloat16),
             pltpu.VMEM((lines, CHUNKS, pack, part), jnp.bfloat16),
             pltpu.VMEM((lines, CHUNKS, pack, part), jnp.bfloat16),
@@ -813,9 +893,11 @@
             pltpu.VMEM((slots, pack), jnp.bfloat16),
             pltpu.VMEM((count, part), jnp.float32),
             dma((6,)), dma((halves,)), dma((halves,)),
-            dma((2,)), dma((2,)), dma((2,)), dma((2,)),
-            dma((devices, 4)), dma((devices,)), dma((devices,)),
-            dma((devices,)), dma((devices,)),
+            dma((CHUNKS,)), dma((CHUNKS,)), dma((CHUNKS,)), dma((CHUNKS,)),
+            dma((lines, PIECES, 2)), dma((lines, PIECES)),
+            dma((lines, PIECES)), dma((lines, PIECES)), dma((CHUNKS,)), dma((CHUNKS,)),
+            dma((lines, 2)), dma((lines, 2)), dma((lines, 2)), dma((lines, 2)),
+            dma((lines, 2)), dma((lines, 2)),
             dma((lines,)), dma((lines,)),
             dma((lines, CHUNKS, 2)), dma((lines, CHUNKS)),
             dma((lines, CHUNKS)), dma((lines, CHUNKS)),
@@ -854,8 +936,9 @@
     paired = parts == 2 and lax.axis_size("groups") == 2 and devices % COLS == 0
     experts_here = gate_up_weight.shape[0] // 2
     tiled = out_weight.shape[0] % (2 * LANES) == 0 and count == LANES
+    tiled = tiled and down_weight.shape[2] // CHUNKS % HEAD == 0 and devices // COLS > 2
     tiled = tiled and down_weight.shape[2] % (2 * CHUNKS * LANES) == 0 and experts_here == devices
-    tiled = tiled and experts_here * (SLOT + CAP) <= out_weight.shape[0] and SLOT * devices == LANES
+    tiled = tiled and SLOT * devices == LANES
     tiled = tiled and gate_up_weight.shape[3] % 64 == 0
     if fits and paired and tiled:
         return block_call(

time: 123 us -> 115 us (0.935); the launches traced: 122 us -> 115 us
  Pallas kernels: 120 us -> 113 us
    pallas_call x1, Pallas kernels: 120 us -> 113 us  [block_call(): pl.pallas_call(functools.partial(block_kernel, devices), out_shape=jax.Sh...]
where the time goes in v2:
time: 115 us
  Pallas kernels  113 us (98%)
  local copies, waits for them, and re-layouts  1.67 us (1%)
    pallas_call x1, Pallas kernels, block_call(): pl.pallas_call(functools.partial(block_kernel, devices), out_shape=jax.Sh...  113 us

profile of v2, /device:TPU:0, one launch (start us, length us, event | category | flops | bytes accessed | tf_op | source)
XLA Modules:
  0.0 114.8 jit_solution(12351032128700647041)
XLA Ops:
  0.0 113.2 %shard_map.82 = bf16[128,1024]{1,0:T(8,128)(2,1)} custom-call(bf16[128,2048]{1,0:T(8,128)(2,1)} %refs_0_.1, bf16[3,128,1024]{2,1,0:T(8,128)(2,1)} %bitcast.5, bf16[256,1024]{1,0:T(8,128)(2,1)} %refs_2_.1, f32[4,2048]{1,0:T(4,128)} %refs_3_.1, bf16[64,2048]{1,0:T(8,128)(2,1)} %bitcast.6, s32[4,128]{1,0:T(4,128)} %bitcast.7, ...), custom_call_target="tpu_custom_call" | custom-call | tf_op jit(solution)/shard_map/pallas_call | solution.py:859
  113.2 1.7 %copy.10 = bf16[128,1024]{1,0:T(8,128)(2,1)} copy(bf16[128,1024]{1,0:T(8,128)(2,1)} %shard_map.82) | data formatting | bytes 524288

commit v3 on v2

--- a/solution.py
+++ b/solution.py
@@ -469,8 +469,8 @@
     devices, start_weights,
     sources, held, own_sem,
     normed, state, meta,
-    near, column, mixed, mixed_in, mine_out, their_out, sent_back, got_back, their_back,
-    near_s, near_r, far_s, far_r, wz_s, wz_r, wy_s, wy_r, mix_s, mix_r,
+    near, relayed, column, mixed, mixed_in, mine_out, their_out, sent_back, got_back, their_back,
+    near_s, near_r, far_s, far_r, way_s, way_r, side_s, wz_s, wz_r, wy_s, wy_r, mix_s, mix_r,
     sum_s, sum_r, back_s, back_r, share_s, share_r,
 ):
     packed_hbm, weight_hbm = sources[1], sources[2]
@@ -530,6 +530,20 @@
     give_far = ((x == 0) & not_top) | ((x == 1) & not_bottom)
     have_far = ((x == 0) & not_bottom) | ((x == 1) & not_top)
 
+    early = pairs // 2
+    give_side = ((x == 1) & not_top) | ((x == 0) & not_bottom)
+    have_side = ((x == 1) & not_bottom) | ((x == 0) & not_top)
+
+    def way_copy(k):
+        src = packed_hbm.at[1:3, :, pl.ds(k * pair, pair)]
+        where = {"dev": jnp.where(x == 1, above, below)}
+        return remote(src, relayed.at[k - early], way_s.at[k - early], way_r.at[k - early], where)
+
+    def side_copy(k):
+        return remote(
+            relayed.at[k - early], near.at[1 - x, k], side_s.at[k - early], far_r.at[k], x_to
+        )
+
     def piece_rows(which, i):
         return pl.ds(pl.multiple_of(which * share + i * piece, SLOT), piece)
 
@@ -559,6 +573,11 @@
         def _():
             wz_copy(z, i, 1, own_piece(i)).start()
 
+    @pl.when(give_side)
+    def _():
+        for k in range(early, pairs):
+            way_copy(k).start()
+
     start_weights()
 
     @pl.when(jnp.logical_not(have_far))
@@ -577,8 +596,8 @@
     def distance(line):
         return jnp.abs(line - z)
 
-    def take(line, onward):
-        for i in range(PIECES):
+    def take(line, onward, pieces=range(PIECES)):
+        for i in pieces:
             wz_copy(line, i, way_of(line)).wait_recv()
 
             @pl.when(onward)
@@ -587,31 +606,33 @@
 
             wy_copy(line, i, group).start()
 
-    def pass_near(k):
+    def take_next(only_busy, pieces):
+        for line in near_lines:
+
+            @pl.when((distance(line) == 1) & (busy(line) if only_busy else jnp.logical_not(busy(line))))
+            def _():
+                take(line, more(line), pieces)
+
+    take_next(True, range(1))
+    take_next(False, range(1))
+    for k in range(early):
         near_copy(k).wait_recv()
 
         @pl.when(give_far)
         def _():
             far_copy(k).start()
 
-    early = pairs // 2
-    for k in range(early):
-        pass_near(k)
-    for line in near_lines:
-
-        @pl.when(distance(line) == 1)
-        def _():
-            take(line, more(line) & jnp.logical_not(busy(line)))
+    take_next(True, range(1, PIECES))
+    take_next(False, range(1, PIECES))
+
+    @pl.when(have_side)
+    def _():
+        for k in range(early, pairs):
+            way_copy(k).wait_recv()
+            side_copy(k).start()
 
     for k in range(early, pairs):
-        pass_near(k)
-    for line in near_lines:
-
-        @pl.when((distance(line) == 1) & busy(line) & more(line))
-        def _():
-            for i in range(PIECES):
-                wz_copy(line, i, way_of(line)).start()
-
+        near_copy(k).wait_recv()
     for i in range(6):
         own_copy(i).wait()
 
@@ -663,7 +684,7 @@
         if k + 1 == early:
             for line in near_lines:
 
-                @pl.when((distance(line) == 2) & jnp.logical_not(busy(line)))
+                @pl.when(distance(line) == 2)
                 def _():
                     take(line, more(line))
 
@@ -713,18 +734,19 @@
         share_copy(*steps[i]).start()
 
     for i, (line, which) in enumerate(steps):
-        if i >= 2:
-            if which == 0:
-
-                @pl.when((distance(line) > 2) | ((distance(line) == 2) & busy(line)))
+        if which == 0 and i == 4:
+            for late in near_lines[1:]:
+
+                @pl.when(distance(late) > 2)
                 def _():
-                    take(line, more(line))
-            else:
-                for n in range(PIECES):
-                    wy_copy(line, n, 1 - group).wait_recv()
+                    take(late, more(late))
+        if which == 1 and i > 1:
+            if i == len(steps) - 1:
+                for n in range(i - 1):
+                    relay(n)
+            for n in range(PIECES):
+                wy_copy(line, n, 1 - group).wait_recv()
         project(line, which)
-        if i >= 2:
-            relay(i - 2)
     relay(len(steps) - 2)
     relay(len(steps) - 1)
 
@@ -766,9 +788,20 @@
         near_copy(k).wait_send()
         mix_copy(k).wait_send()
 
-        @pl.when(give_far)
-        def _():
-            far_copy(k).wait_send()
+        if k < early:
+
+            @pl.when(give_far)
+            def _():
+                far_copy(k).wait_send()
+        else:
+
+            @pl.when(give_side)
+            def _():
+                way_copy(k).wait_send()
+
+            @pl.when(have_side)
+            def _():
+                side_copy(k).wait_send()
 
     for i in range(PIECES):
 
@@ -796,9 +829,9 @@
 def block_kernel(devices, *refs):
     sources, gate_up, down, out = refs[:6], refs[6], refs[7], refs[8]
     held, normed, state, meta, wide = refs[9:14], refs[14], refs[15], refs[16], refs[17]
-    front_buffers, expert_buffers = refs[18:27], refs[27:43]
-    own_sem, gu_sem, dn_sem = refs[43:46]
-    front_sems, expert_sems = refs[46:62], refs[62:]
+    front_buffers, expert_buffers = refs[18:28], refs[28:44]
+    own_sem, gu_sem, dn_sem = refs[44:47]
+    front_sems, expert_sems = refs[47:66], refs[66:]
     gu, dn, raised = expert_buffers[5:8]
     squeeze, grow = expert_buffers[13:15]
     halves = gate_up.shape[0]
@@ -868,6 +901,7 @@
             pltpu.VMEM((router_weight.shape[1], count), jnp.float32),
             pltpu.VMEM((devices, slots + pack, half), jnp.bfloat16),
             pltpu.VMEM((2, CHUNKS, 2, count, part), jnp.bfloat16),
+            pltpu.VMEM((CHUNKS // 2, 2, count, part), jnp.bfloat16),
             pltpu.VMEM((lines, shard, half), jnp.bfloat16),
             pltpu.VMEM((count, half), jnp.bfloat16),
             pltpu.VMEM((count, half), jnp.bfloat16),
@@ -894,6 +928,7 @@
             pltpu.VMEM((count, part), jnp.float32),
             dma((6,)), dma((halves,)), dma((halves,)),
             dma((CHUNKS,)), dma((CHUNKS,)), dma((CHUNKS,)), dma((CHUNKS,)),
+            dma((CHUNKS // 2,)), dma((CHUNKS // 2,)), dma((CHUNKS // 2,)),
             dma((lines, PIECES, 2)), dma((lines, PIECES)),
             dma((lines, PIECES)), dma((lines, PIECES)), dma((CHUNKS,)), dma((CHUNKS,)),
             dma((lines, 2)), dma((lines, 2)), dma((lines, 2)), dma((lines, 2)),

time: 115 us -> 108 us (0.939)
  Pallas kernels: 113 us -> 106 us
    pallas_call x1, Pallas kernels: 113 us -> 106 us  [block_call(): pl.pallas_call(functools.partial(block_kernel, devices), out_shape=jax.Sh...]
where the time goes in v3:
time: 108 us
  Pallas kernels  106 us (98%)
  local copies, waits for them, and re-layouts  1.67 us (2%)
    pallas_call x1, Pallas kernels, block_call(): pl.pallas_call(functools.partial(block_kernel, devices), out_shape=jax.Sh...  106 us

profile of v3, /device:TPU:0, one launch (start us, length us, event | category | flops | bytes accessed | tf_op | source)
XLA Modules:
  0.0 107.7 jit_solution(3368766808792861022)
XLA Ops:
  0.0 106.0 %shard_map.82 = bf16[128,1024]{1,0:T(8,128)(2,1)} custom-call(bf16[128,2048]{1,0:T(8,128)(2,1)} %refs_0_.1, bf16[3,128,1024]{2,1,0:T(8,128)(2,1)} %bitcast.5, bf16[256,1024]{1,0:T(8,128)(2,1)} %refs_2_.1, f32[4,2048]{1,0:T(4,128)} %refs_3_.1, bf16[64,2048]{1,0:T(8,128)(2,1)} %bitcast.6, s32[4,128]{1,0:T(4,128)} %bitcast.7, ...), custom_call_target="tpu_custom_call" | custom-call | tf_op jit(solution)/shard_map/pallas_call | solution.py:892
  106.0 1.7 %copy.10 = bf16[128,1024]{1,0:T(8,128)(2,1)} copy(bf16[128,1024]{1,0:T(8,128)(2,1)} %shard_map.82) | data formatting | bytes 524288

commit v4 on v3

--- a/solution.py
+++ b/solution.py
@@ -80,10 +80,10 @@
     return value
 
 
-def line_order(lines, nearest):
+def line_order(lines, nearest, inner=False):
     rows = []
     for z in range(lines):
-        lower = z < lines - 1 - z
+        lower = (z < lines - 1 - z) != inner
         others = [line for line in range(lines) if line != z]
         sign = 1 if nearest else -1
         rows.append(sorted(others, key=lambda line: (sign * abs(line - z), (line > z) == lower)))
@@ -94,7 +94,7 @@
     devices, weight_copies,
     normed, meta, state, modulation, wide,
     out,
-    tok, got_packed, got_rows, got_sum, disp, gu, dn, raised, hid_own, hid_other,
+    tok, got_packed, got_rows, got_sum, disp, gu, dn, hid_own, hid_other,
     got_meta, pick, gated, squeeze, grow, acc,
     meta_s, meta_r, z_s, z_r, x_s, x_r, core_s, core_r, hid_s, hid_r, rx_s, rx_r, rz_s, rz_r,
 ):
@@ -106,9 +106,8 @@
     lines = devices // COLS
     count, width = normed.shape
     half = width // 2
-    local = raised.shape[0]
+    local = hid_own.shape[0]
     hidden = gu.shape[2]
-    both_hidden = 2 * hidden
     slots = local * SLOT
     pack = local * CAP
     rows = devices * SLOT
@@ -126,7 +125,7 @@
     core_to = {"sub": other}
     not_top = z < lines - 1
     not_bottom = z > 0
-    near_lines = [choose(z, table) for table in line_order(lines, True)]
+    near_lines = [choose(z, table) for table in line_order(lines, True, True)]
     far_lines = [choose(z, table) for table in line_order(lines, False)]
 
     def lanes_of(c):
@@ -253,16 +252,25 @@
             left, right, (((1,), (1,)), ((), ())), preferred_element_type=jnp.float32
         )
 
-    def raise_part(e, c):
-        total = raised[e]
-        for side in range(2):
-            lanes = pl.ds(pl.multiple_of(side * half + c * wide_chunk, wide_chunk), wide_chunk)
-            weight = jnp.concatenate(
-                [gu[2 * e, 0, :, lanes], gu[2 * e + 1, 0, :, lanes],
-                 gu[2 * e, 1, :, lanes], gu[2 * e + 1, 1, :, lanes]], axis=0
-            )
-            total = total + across_rows(disp[side, c, e], weight)
-        return total
+    def raise_expert(e):
+        sums = []
+        for g in range(2):
+            for b in range(2):
+                total = None
+                for c in range(chunks):
+                    for side in range(2):
+                        start = side * half + c * wide_chunk
+                        piece = across_rows(
+                            gu[2 * e + b, g, :, start:start + wide_chunk], disp[side, c, e]
+                        )
+                        total = piece if total is None else total + piece
+                sums.append(total)
+        for b in range(2):
+            gate = sums[b]
+            hid_own[e, b * hidden:(b + 1) * hidden] = (
+                gate * jax.nn.sigmoid(gate) * sums[2 + b]
+            ).astype(jnp.bfloat16)
+        hid_copy(e).start()
 
     def hid_copy(e):
         return remote(hid_own.at[e], hid_other.at[e], hid_s.at[e], hid_r.at[e], core_to)
@@ -284,24 +292,6 @@
     lax.fori_loop(0, 2 * local, weight_wait, 0)
 
     def step(t, carry):
-        ready = t - lines
-
-        def raise_some(i):
-            first, last = i * local // (2 * lines), (i + 1) * local // (2 * lines)
-
-            @pl.when(ready >= 0)
-            def _():
-                if i == 0:
-                    arrived(ready)
-                for e in range(first, last):
-                    raised[e] = raise_part(e, ready)
-
-        @pl.when(t + 1 < chunks)
-        def _():
-            own_send(t + 1)
-            own_step(t + 1)
-
-        raise_some(0)
         for j, line in enumerate(near_lines):
             c = t - jnp.abs(line - z) + 1
 
@@ -309,13 +299,17 @@
             def _():
                 line_step(line, c)
 
-            raise_some(1 + j)
+            if j == 0:
+
+                @pl.when(t + 1 < chunks)
+                def _():
+                    own_send(t + 1)
+                    own_step(t + 1)
 
         @pl.when(t < chunks)
         def _():
             x_step(z, t)
 
-        raise_some(lines)
         for j, line in enumerate(near_lines):
             c = t - jnp.abs(line - z)
 
@@ -323,42 +317,33 @@
             def _():
                 x_step(line, c)
 
-            raise_some(lines + 1 + j)
         return carry
 
     lax.fori_loop(0, chunks + lines - 1, step, 0)
-    arrived(chunks - 1)
-
-    def last_raise(e, carry):
-        total = raise_part(e, chunks - 1)
-        gate = total[:, :both_hidden]
-        hid_own[e] = (gate * jax.nn.sigmoid(gate) * total[:, both_hidden:]).astype(jnp.bfloat16)
-        hid_copy(e).start()
+    for c in range(chunks):
+        arrived(c)
+
+    def lower_expert(e):
+        hid_copy(e).wait_recv()
+        mine = pl.ds(pl.multiple_of(part * hidden, SLOT), hidden)
+        theirs = pl.ds(pl.multiple_of(other * hidden, SLOT), hidden)
+        left = jnp.concatenate([hid_own[e], hid_other[e]], axis=0)
+        right = jnp.concatenate(
+            [dn[2 * e, mine], dn[2 * e + 1, mine], dn[2 * e, theirs], dn[2 * e + 1, theirs]], axis=0
+        )
+        wide[e, :rows] = lax.dot_general(
+            left, right, (((0,), (0,)), ((), ())), preferred_element_type=jnp.float32
+        ).astype(jnp.bfloat16)
+
+    raise_expert(0)
+
+    def both_ways(e, carry):
+        raise_expert(e)
+        lower_expert(e - 1)
         return carry
 
-    lax.fori_loop(0, local, last_raise, 0)
-
-    group = 2 * wide_chunk
-
-    def lower(g):
-        lanes = slice(g * group, (g + 1) * group)
-
-        def one(e, carry):
-            if g == 0:
-                hid_copy(e).wait_recv()
-            mine = pl.ds(pl.multiple_of(part * hidden, SLOT), hidden)
-            theirs = pl.ds(pl.multiple_of(other * hidden, SLOT), hidden)
-            left = jnp.concatenate([hid_own[e], hid_other[e]], axis=1)
-            right = jnp.concatenate(
-                [dn[2 * e, mine, lanes], dn[2 * e + 1, mine, lanes],
-                 dn[2 * e, theirs, lanes], dn[2 * e + 1, theirs, lanes]], axis=0
-            )
-            wide[e, :rows, lanes] = jnp.dot(
-                left, right, preferred_element_type=jnp.float32
-            ).astype(jnp.bfloat16)
-            return carry
-
-        lax.fori_loop(0, local, one, 0)
+    lax.fori_loop(1, local, both_ways, 0)
+    lower_expert(local - 1)
 
     def result_rows(s, q):
         return wide[:local, slot_rows(s), lanes_of(q)].reshape(slots, wide_chunk)
@@ -405,11 +390,7 @@
         tok[line, q] = acc[...].astype(jnp.bfloat16)
         rz_copy(line, q, way).start()
 
-    for g in range(half // group):
-        lower(g)
-        for q in range(2 * g, 2 * g + 2):
-            give(far_lines[0], q)
-    for line in far_lines[1:] + [z]:
+    for line in far_lines + [z]:
         lax.fori_loop(0, chunks, lambda q, carry, line=line: (give(line, q), carry)[1], 0)
     for line in near_lines:
         low = line < z
@@ -829,11 +810,11 @@
 def block_kernel(devices, *refs):
     sources, gate_up, down, out = refs[:6], refs[6], refs[7], refs[8]
     held, normed, state, meta, wide = refs[9:14], refs[14], refs[15], refs[16], refs[17]
-    front_buffers, expert_buffers = refs[18:28], refs[28:44]
-    own_sem, gu_sem, dn_sem = refs[44:47]
-    front_sems, expert_sems = refs[47:66], refs[66:]
-    gu, dn, raised = expert_buffers[5:8]
-    squeeze, grow = expert_buffers[13:15]
+    front_buffers, expert_buffers = refs[18:28], refs[28:43]
+    own_sem, gu_sem, dn_sem = refs[43:46]
+    front_sems, expert_sems = refs[46:65], refs[65:]
+    gu, dn = expert_buffers[5:7]
+    squeeze, grow = expert_buffers[12:14]
     halves = gate_up.shape[0]
 
     def weight_copies(h):
@@ -849,7 +830,6 @@
             return carry
 
         lax.fori_loop(0, halves, one, 0)
-        raised[...] = jnp.zeros_like(raised)
         for ref, axis in ((squeeze, 0), (grow, 1)):
             packed = lax.broadcasted_iota(jnp.int32, ref.shape, axis)
             slot = lax.broadcasted_iota(jnp.int32, ref.shape, 1 - axis)
@@ -917,9 +897,8 @@
             pltpu.VMEM((2, CHUNKS, local, rows, part), jnp.bfloat16),
             pltpu.VMEM(gate_up_weight.shape, jnp.bfloat16),
             pltpu.VMEM(down_weight.shape, jnp.bfloat16),
-            pltpu.VMEM((local, rows, 4 * hidden), jnp.float32),
-            pltpu.VMEM((local, rows, 2 * hidden), jnp.bfloat16),
-            pltpu.VMEM((local, rows, 2 * hidden), jnp.bfloat16),
+            pltpu.VMEM((local, 2 * hidden, rows), jnp.bfloat16),
+            pltpu.VMEM((local, 2 * hidden, rows), jnp.bfloat16),
             pltpu.VMEM((lines, COLS * local, count), jnp.float32),
             pltpu.VMEM((lines, slots + pack, count), jnp.bfloat16),
             pltpu.VMEM((lines, slots + pack, count), jnp.bfloat16),

time: 108 us -> 106 us (0.981)
  Pallas kernels: 106 us -> 104 us
    pallas_call x1, Pallas kernels: 106 us -> 104 us  [block_call(): pl.pallas_call(functools.partial(block_kernel, devices), out_shape=jax.Sh...]
where the time goes in v4:
time: 106 us
  Pallas kernels  104 us (98%)
  local copies, waits for them, and re-layouts  1.67 us (2%)
    pallas_call x1, Pallas kernels, block_call(): pl.pallas_call(functools.partial(block_kernel, devices), out_shape=jax.Sh...  104 us

profile of v4, /device:TPU:0, one launch (start us, length us, event | category | flops | bytes accessed | tf_op | source)
XLA Modules:
  0.0 105.5 jit_solution(12386265571556822151)
XLA Ops:
  0.0 103.9 %shard_map.82 = bf16[128,1024]{1,0:T(8,128)(2,1)} custom-call(bf16[128,2048]{1,0:T(8,128)(2,1)} %refs_0_.1, bf16[3,128,1024]{2,1,0:T(8,128)(2,1)} %bitcast.5, bf16[256,1024]{1,0:T(8,128)(2,1)} %refs_2_.1, f32[4,2048]{1,0:T(4,128)} %refs_3_.1, bf16[64,2048]{1,0:T(8,128)(2,1)} %bitcast.6, s32[4,128]{1,0:T(4,128)} %bitcast.7, ...), custom_call_target="tpu_custom_call" | custom-call | tf_op jit(solution)/shard_map/pallas_call | solution.py:872
  103.9 1.7 %copy.10 = bf16[128,1024]{1,0:T(8,128)(2,1)} copy(bf16[128,1024]{1,0:T(8,128)(2,1)} %shard_map.82) | data formatting | bytes 524288

commit v5 on v4

--- a/solution.py
+++ b/solution.py
@@ -68,7 +68,8 @@
 SLOT = 16
 COLS = 2
 CHUNKS = 4
-PIECES = 2
+PIECES = 4
+LAG = 2
 VMEM_BYTES = 66 * 1000 * 1000
 MESH = pl.DeviceIdType.MESH
 
@@ -94,7 +95,7 @@
     devices, weight_copies,
     normed, meta, state, modulation, wide,
     out,
-    tok, got_packed, got_rows, got_sum, disp, gu, dn, hid_own, hid_other,
+    tok, got_packed, got_rows, got_sum, disp, gu, dn, raised, hid_own, hid_other,
     got_meta, pick, gated, squeeze, grow, acc,
     meta_s, meta_r, z_s, z_r, x_s, x_r, core_s, core_r, hid_s, hid_r, rx_s, rx_r, rz_s, rz_r,
 ):
@@ -179,6 +180,8 @@
     own_send(0)
     for line in near_lines:
         meta_copy(line).start()
+    for c in range(1, chunks):
+        own_send(c)
 
     before = (
         lax.broadcasted_iota(jnp.int32, (count, count), 0)
@@ -252,37 +255,51 @@
             left, right, (((1,), (1,)), ((), ())), preferred_element_type=jnp.float32
         )
 
-    def raise_expert(e):
+    def raise_side(e, side):
         sums = []
         for g in range(2):
             for b in range(2):
                 total = None
                 for c in range(chunks):
-                    for side in range(2):
-                        start = side * half + c * wide_chunk
-                        piece = across_rows(
-                            gu[2 * e + b, g, :, start:start + wide_chunk], disp[side, c, e]
-                        )
-                        total = piece if total is None else total + piece
+                    start = side * half + c * wide_chunk
+                    piece = across_rows(
+                        gu[2 * e + b, g, :, start:start + wide_chunk], disp[side, c, e]
+                    )
+                    total = piece if total is None else total + piece
                 sums.append(total)
+        return sums
+
+    def raise_first(e, carry):
+        for n, total in enumerate(raise_side(e, 1)):
+            raised[e, n * hidden:(n + 1) * hidden] = total
+        return carry
+
+    def raise_second(e, carry):
+        sums = [
+            total + raised[e, n * hidden:(n + 1) * hidden]
+            for n, total in enumerate(raise_side(e, 0))
+        ]
         for b in range(2):
             gate = sums[b]
             hid_own[e, b * hidden:(b + 1) * hidden] = (
                 gate * jax.nn.sigmoid(gate) * sums[2 + b]
             ).astype(jnp.bfloat16)
         hid_copy(e).start()
+        return carry
 
     def hid_copy(e):
         return remote(hid_own.at[e], hid_other.at[e], hid_s.at[e], hid_r.at[e], core_to)
 
-    def arrived(c):
-        for s in range(devices):
-            core_copy(other, s, c).wait_recv()
+    def arrived():
+        for c in range(chunks):
+            for s in range(devices):
+                core_copy(other, s, c).wait_recv()
 
     routing(
         z, meta[expert_rows(z * COLS * local, x)], meta[expert_rows(z * COLS * local, 1 - x)]
     )
-    own_step(0)
+    for c in range(chunks):
+        own_step(c)
 
     def weight_wait(h, carry):
         for copy in weight_copies(h):
@@ -292,26 +309,19 @@
     lax.fori_loop(0, 2 * local, weight_wait, 0)
 
     def step(t, carry):
-        for j, line in enumerate(near_lines):
-            c = t - jnp.abs(line - z) + 1
+        for line in near_lines:
+            c = t - (jnp.abs(line - z) - 1) * chunks
 
             @pl.when((c >= 0) & (c < chunks))
             def _():
                 line_step(line, c)
 
-            if j == 0:
-
-                @pl.when(t + 1 < chunks)
-                def _():
-                    own_send(t + 1)
-                    own_step(t + 1)
-
-        @pl.when(t < chunks)
-        def _():
-            x_step(z, t)
-
-        for j, line in enumerate(near_lines):
-            c = t - jnp.abs(line - z)
+        @pl.when((t >= 1) & (t < 1 + chunks))
+        def _():
+            x_step(z, t - 1)
+
+        for line in near_lines:
+            c = t - LAG - (jnp.abs(line - z) - 1) * chunks
 
             @pl.when((c >= 0) & (c < chunks))
             def _():
@@ -319,31 +329,51 @@
 
         return carry
 
-    lax.fori_loop(0, chunks + lines - 1, step, 0)
-    for c in range(chunks):
-        arrived(c)
-
-    def lower_expert(e):
-        hid_copy(e).wait_recv()
-        mine = pl.ds(pl.multiple_of(part * hidden, SLOT), hidden)
-        theirs = pl.ds(pl.multiple_of(other * hidden, SLOT), hidden)
-        left = jnp.concatenate([hid_own[e], hid_other[e]], axis=0)
-        right = jnp.concatenate(
-            [dn[2 * e, mine], dn[2 * e + 1, mine], dn[2 * e, theirs], dn[2 * e + 1, theirs]], axis=0
-        )
-        wide[e, :rows] = lax.dot_general(
-            left, right, (((0,), (0,)), ((), ())), preferred_element_type=jnp.float32
-        ).astype(jnp.bfloat16)
-
-    raise_expert(0)
-
-    def both_ways(e, carry):
-        raise_expert(e)
-        lower_expert(e - 1)
-        return carry
-
-    lax.fori_loop(1, local, both_ways, 0)
-    lower_expert(local - 1)
+    span = chunks * (lines - 1) + LAG
+    lax.fori_loop(0, span - 2, step, 0)
+    first, second = local * 3 // 8, local * 5 // 8
+
+    def early_raise(start, stop):
+        @pl.when(part == 0)
+        def _():
+            if start == 0:
+                arrived()
+            lax.fori_loop(start, stop, raise_first, 0)
+
+    early_raise(0, first)
+    step(span - 2, 0)
+    early_raise(first, second)
+    step(span - 1, 0)
+    early_raise(second, local)
+
+    @pl.when(part == 1)
+    def _():
+        lax.fori_loop(0, local, raise_first, 0)
+        arrived()
+
+    lax.fori_loop(0, local, raise_second, 0)
+
+    group = 2 * wide_chunk
+
+    def lower(g):
+        lanes = slice(g * group, (g + 1) * group)
+
+        def one(e, carry):
+            if g == 0:
+                hid_copy(e).wait_recv()
+            mine = pl.ds(pl.multiple_of(part * hidden, SLOT), hidden)
+            theirs = pl.ds(pl.multiple_of(other * hidden, SLOT), hidden)
+            left = jnp.concatenate([hid_own[e], hid_other[e]], axis=0)
+            right = jnp.concatenate(
+                [dn[2 * e, mine, lanes], dn[2 * e + 1, mine, lanes],
+                 dn[2 * e, theirs, lanes], dn[2 * e + 1, theirs, lanes]], axis=0
+            )
+            wide[e, :rows, lanes] = lax.dot_general(
+                left, right, (((0,), (0,)), ((), ())), preferred_element_type=jnp.float32
+            ).astype(jnp.bfloat16)
+            return carry
+
+        lax.fori_loop(0, local, one, 0)
 
     def result_rows(s, q):
         return wide[:local, slot_rows(s), lanes_of(q)].reshape(slots, wide_chunk)
@@ -390,8 +420,13 @@
         tok[line, q] = acc[...].astype(jnp.bfloat16)
         rz_copy(line, q, way).start()
 
-    for line in far_lines + [z]:
-        lax.fori_loop(0, chunks, lambda q, carry, line=line: (give(line, q), carry)[1], 0)
+    for g in range(half // group):
+        lower(g)
+        for q in range(2 * g, 2 * g + 2):
+            give(far_lines[0], q)
+    def give_all(line):
+        lax.fori_loop(0, chunks, lambda q, carry: (give(line, q), carry)[1], 0)
+
     for line in near_lines:
         low = line < z
 
@@ -400,7 +435,29 @@
             for c in range(chunks):
                 z_copy(line, c, jnp.where(low, 0, 1)).wait_send()
 
-    for line in far_lines:
+    far_end = (z == 0) | (z == lines - 1)
+
+    @pl.when(far_end)
+    def _():
+        for q in range(2):
+            pass_on(far_lines[0], q)
+
+    give_all(far_lines[1])
+
+    @pl.when(far_end)
+    def _():
+        for q in range(2, chunks):
+            pass_on(far_lines[0], q)
+
+    for line in far_lines[2:] + [z]:
+        give_all(line)
+
+    @pl.when(jnp.logical_not(far_end))
+    def _():
+        for q in range(chunks):
+            pass_on(far_lines[0], q)
+
+    for line in far_lines[1:]:
         lax.fori_loop(0, chunks, lambda q, carry, line=line: (pass_on(line, q), carry)[1], 0)
     for q in range(chunks):
         gather_here(z, q)
@@ -488,11 +545,11 @@
     def greet(where):
         pl.semaphore_signal(barrier, inc=1, device_id=where, device_id_type=MESH)
 
-    for where in (x_to, y_to, core_to):
+    for where in (x_to, y_to, core_to, {**x_to, **core_to}):
         greet(where)
     for line in near_lines:
         greet({"dev": line * COLS + x})
-    pl.semaphore_wait(barrier, lines + 2)
+    pl.semaphore_wait(barrier, lines + 3)
 
     def remote(src, dst, send, recv, where):
         return pltpu.make_async_remote_copy(
@@ -594,8 +651,8 @@
             def _():
                 take(line, more(line), pieces)
 
-    take_next(True, range(1))
-    take_next(False, range(1))
+    take_next(True, range(PIECES // 2))
+    take_next(False, range(PIECES // 2))
     for k in range(early):
         near_copy(k).wait_recv()
 
@@ -603,8 +660,8 @@
         def _():
             far_copy(k).start()
 
-    take_next(True, range(1, PIECES))
-    take_next(False, range(1, PIECES))
+    take_next(True, range(PIECES // 2, PIECES))
+    take_next(False, range(PIECES // 2, PIECES))
 
     @pl.when(have_side)
     def _():
@@ -669,6 +726,13 @@
                 def _():
                     take(line, more(line))
 
+    last = near_lines[-1]
+    far_last = distance(last) > 2
+
+    @pl.when(far_last)
+    def _():
+        take(last, more(last))
+
     for k in range(pairs):
         mix_copy(k).wait_recv()
 
@@ -696,7 +760,15 @@
             share_s.at[line, which], share_r.at[line, which], core_to,
         )
 
-    def project(line, which):
+    def direct_copy(which):
+        place = place_of(which)
+        return remote(
+            sent_back.at[last, place], their_back.at[last, place],
+            share_s.at[last, which], share_r.at[last, which],
+            {"dev": z * COLS + (1 - x), "sub": 1 - part},
+        )
+
+    def project(line, which, direct=False):
         place = place_of(which)
         block = column[line, pl.ds(pl.multiple_of(place * share, SLOT), share), :]
         both = jnp.concatenate([mixed_in[...], mixed[...]], axis=0)
@@ -705,37 +777,24 @@
         )
         sent_back[line, place] = product[:count].astype(jnp.bfloat16)
         back_copy(line, which).start()
+        if direct:
+            direct_copy(which).start()
         mine_out[line, place] = product[count:]
         sum_copy(line, which).start()
 
-    steps = [(line, which) for line in [z] + near_lines for which in range(2)]
-
-    def relay(i):
-        back_copy(*steps[i]).wait_recv()
-        share_copy(*steps[i]).start()
-
-    for i, (line, which) in enumerate(steps):
-        if which == 0 and i == 4:
-            for late in near_lines[1:]:
-
-                @pl.when(distance(late) > 2)
-                def _():
-                    take(late, more(late))
-        if which == 1 and i > 1:
-            if i == len(steps) - 1:
-                for n in range(i - 1):
-                    relay(n)
-            for n in range(PIECES):
-                wy_copy(line, n, 1 - group).wait_recv()
-        project(line, which)
-    relay(len(steps) - 2)
-    relay(len(steps) - 1)
-
-    square = jnp.zeros((count, 1), jnp.float32)
-    for line, which in steps:
+    def halves_in(line):
+        for n in range(PIECES):
+            wy_copy(line, n, 1 - group).wait_recv()
+
+    def last_step():
+        halves_in(last)
+        project(last, 1, True)
+
+    def add_up(line, which):
         place = place_of(which)
         sum_copy(line, which).wait_recv()
         share_copy(line, which).wait_recv()
+        partial = jnp.zeros((count, share), jnp.float32)
         for column_of, total in (
             (x, mine_out[line, place] + their_out[line, place]),
             (
@@ -748,7 +807,37 @@
             lanes = pl.ds(pl.multiple_of(start, LANES), share)
             value = tokens[:, lanes].astype(jnp.float32) + (1.0 + modulation[0:1, lanes]) * total
             state[:, lanes] = value
-            square = square + jnp.sum(value * value, -1, keepdims=True)
+            partial = partial + value * value
+        return partial
+
+    steps = [(line, which) for line in [z] + near_lines[:-1] for which in range(2)]
+    project(z, 0)
+    project(z, 1)
+    for line in near_lines[:-1]:
+        project(line, 0)
+        halves_in(line)
+        project(line, 1)
+    project(last, 0, True)
+
+    @pl.when(jnp.logical_not(far_last))
+    def _():
+        last_step()
+
+    for line, which in steps:
+        back_copy(line, which).wait_recv()
+        share_copy(line, which).start()
+    squares = jnp.zeros((count, share), jnp.float32)
+    for line, which in steps:
+        squares = squares + add_up(line, which)
+
+    @pl.when(far_last)
+    def _():
+        last_step()
+
+    for which in range(2):
+        back_copy(last, which).wait_recv()
+        squares = squares + add_up(last, which)
+    square = jnp.sum(squares, -1, keepdims=True)
     scale = lax.rsqrt(square / width + EPS)
     for s in range(devices):
         lanes = slice(s * shard, (s + 1) * shard)
@@ -801,7 +890,7 @@
                 wz_copy(line, i, way_of(line)).wait_send()
 
             wy_copy(line, i, group).wait_send()
-    for line, which in steps:
+    for line, which in steps + [(last, 0), (last, 1)]:
         sum_copy(line, which).wait_send()
         back_copy(line, which).wait_send()
         share_copy(line, which).wait_send()
@@ -810,11 +899,11 @@
 def block_kernel(devices, *refs):
     sources, gate_up, down, out = refs[:6], refs[6], refs[7], refs[8]
     held, normed, state, meta, wide = refs[9:14], refs[14], refs[15], refs[16], refs[17]
-    front_buffers, expert_buffers = refs[18:28], refs[28:43]
-    own_sem, gu_sem, dn_sem = refs[43:46]
-    front_sems, expert_sems = refs[46:65], refs[65:]
+    front_buffers, expert_buffers = refs[18:28], refs[28:44]
+    own_sem, gu_sem, dn_sem = refs[44:47]
+    front_sems, expert_sems = refs[47:66], refs[66:]
     gu, dn = expert_buffers[5:7]
-    squeeze, grow = expert_buffers[12:14]
+    squeeze, grow = expert_buffers[13:15]
     halves = gate_up.shape[0]
 
     def weight_copies(h):
@@ -897,6 +986,7 @@
             pltpu.VMEM((2, CHUNKS, local, rows, part), jnp.bfloat16),
             pltpu.VMEM(gate_up_weight.shape, jnp.bfloat16),
             pltpu.VMEM(down_weight.shape, jnp.bfloat16),
+            pltpu.VMEM((local, 4 * hidden, rows), jnp.float32),
             pltpu.VMEM((local, 2 * hidden, rows), jnp.bfloat16),
             pltpu.VMEM((local, 2 * hidden, rows), jnp.bfloat16),
             pltpu.VMEM((lines, COLS * local, count), jnp.float32),
@@ -950,7 +1040,7 @@
     paired = parts == 2 and lax.axis_size("groups") == 2 and devices % COLS == 0
     experts_here = gate_up_weight.shape[0] // 2
     tiled = out_weight.shape[0] % (2 * LANES) == 0 and count == LANES
-    tiled = tiled and down_weight.shape[2] // CHUNKS % HEAD == 0 and devices // COLS > 2
+    tiled = tiled and down_weight.shape[2] // CHUNKS % HEAD == 0 and devices == 4 * COLS
     tiled = tiled and down_weight.shape[2] % (2 * CHUNKS * LANES) == 0 and experts_here == devices
     tiled = tiled and SLOT * devices == LANES
     tiled = tiled and gate_up_weight.shape[3] % 64 == 0

time: 106 us -> 98.4 us (0.928)
  Pallas kernels: 104 us -> 96.6 us
    pallas_call x1, Pallas kernels: 104 us -> 96.6 us  [block_call(): pl.pallas_call(functools.partial(block_kernel, devices), out_shape=jax.Sh...]
where the time goes in v5:
time: 98.4 us; the launch traced here: 98.3 us
  Pallas kernels  96.6 us (98%)
  local copies, waits for them, and re-layouts  1.67 us (2%)
    pallas_call x1, Pallas kernels, block_call(): pl.pallas_call(functools.partial(block_kernel, devices), out_shape=jax.Sh...  96.6 us

profile of v5, /device:TPU:0, one launch (start us, length us, event | category | flops | bytes accessed | tf_op | source)
XLA Modules:
  0.0 98.3 jit_solution(18147115589695305673)
XLA Ops:
  0.0 96.6 %shard_map.82 = bf16[128,1024]{1,0:T(8,128)(2,1)} custom-call(bf16[128,2048]{1,0:T(8,128)(2,1)} %refs_0_.1, bf16[3,128,1024]{2,1,0:T(8,128)(2,1)} %bitcast.5, bf16[256,1024]{1,0:T(8,128)(2,1)} %refs_2_.1, f32[4,2048]{1,0:T(4,128)} %refs_3_.1, bf16[64,2048]{1,0:T(8,128)(2,1)} %bitcast.6, s32[4,128]{1,0:T(4,128)} %bitcast.7, ...), custom_call_target="tpu_custom_call" | custom-call | tf_op jit(solution)/shard_map/pallas_call | solution.py:961
  96.6 1.7 %copy.10 = bf16[128,1024]{1,0:T(8,128)(2,1)} copy(bf16[128,1024]{1,0:T(8,128)(2,1)} %shard_map.82) | data formatting | bytes 524288

commit v6 on v5

--- a/solution.py
+++ b/solution.py
@@ -70,6 +70,7 @@
 CHUNKS = 4
 PIECES = 4
 LAG = 2
+PAIR = 256
 VMEM_BYTES = 66 * 1000 * 1000
 MESH = pl.DeviceIdType.MESH
 
@@ -507,12 +508,12 @@
     devices, start_weights,
     sources, held, own_sem,
     normed, state, meta,
-    near, relayed, column, mixed, mixed_in, mine_out, their_out, sent_back, got_back, their_back,
-    near_s, near_r, far_s, far_r, way_s, way_r, side_s, wz_s, wz_r, wy_s, wy_r, mix_s, mix_r,
+    window, queries, column, mixed, mine_out, their_out, sent_back, got_back, their_back,
+    pair_s, pair_r, query_s, query_r, early_s, late_s, edge_r, wz_s, wz_r, wy_s, wy_r, mix_s, mix_r,
     sum_s, sum_r, back_s, back_r, share_s, share_r,
 ):
     packed_hbm, weight_hbm = sources[1], sources[2]
-    tokens, packed, modulation, router, ids = held
+    tokens, modulation, router, ids = held
     me = lax.axis_index("dev")
     part = lax.axis_index("sub")
     group = lax.axis_index("groups")
@@ -523,13 +524,20 @@
     shard = column.shape[1]
     share = shard // 2
     piece = share // PIECES
-    pairs, pair = near.shape[1], near.shape[4]
-    targets = (tokens, packed, column.at[z], modulation, router, ids)
+    heads = window.shape[3]
+    pairs = heads // PAIR
+    ours = pl.ds(pl.multiple_of(x * heads, heads), heads)
+    theirs = pl.ds(pl.multiple_of((1 - x) * heads, heads), heads)
+    own_parts = (
+        (packed_hbm.at[1:3, :, ours], window.at[1 + x]), (packed_hbm.at[0, :, ours], queries.at[x]),
+        (weight_hbm, column.at[z]), (sources[0], tokens), (sources[3], modulation),
+        (sources[4], router), (sources[5], ids),
+    )
 
     def own_copy(i):
-        return pltpu.make_async_copy(sources[i], targets[i], own_sem.at[i])
-
-    for i in (1, 2, 0, 3, 4, 5):
+        return pltpu.make_async_copy(*own_parts[i], own_sem.at[i])
+
+    for i in range(len(own_parts)):
         own_copy(i).start()
     not_top = z < lines - 1
     not_bottom = z > 0
@@ -557,30 +565,36 @@
             device_id=where, device_id_type=MESH,
         )
 
-    def near_copy(k):
-        src = packed_hbm.at[1:3, :, pl.ds(k * pair, pair)]
-        return remote(src, near.at[x, k], near_s.at[k], near_r.at[k], x_to)
-
-    def far_copy(k):
-        where = {"dev": jnp.where(x == 0, above, below)}
-        return remote(near.at[1 - x, k], near.at[x, k], far_s.at[k], far_r.at[k], where)
-
-    give_far = ((x == 0) & not_top) | ((x == 1) & not_bottom)
-    have_far = ((x == 0) & not_bottom) | ((x == 1) & not_top)
-
-    early = pairs // 2
-    give_side = ((x == 1) & not_top) | ((x == 0) & not_bottom)
-    have_side = ((x == 1) & not_bottom) | ((x == 0) & not_top)
-
-    def way_copy(k):
-        src = packed_hbm.at[1:3, :, pl.ds(k * pair, pair)]
-        where = {"dev": jnp.where(x == 1, above, below)}
-        return remote(src, relayed.at[k - early], way_s.at[k - early], way_r.at[k - early], where)
-
-    def side_copy(k):
-        return remote(
-            relayed.at[k - early], near.at[1 - x, k], side_s.at[k - early], far_r.at[k], x_to
-        )
+    def part_lanes(base, k):
+        return pl.ds(pl.multiple_of(base * heads + k * PAIR, PAIR), PAIR)
+
+    def pair_copy(k):
+        return remote(
+            packed_hbm.at[1:3, :, part_lanes(1 - x, k)], window.at[1 + x, :, :, part_lanes(0, k)],
+            pair_s.at[k], pair_r.at[k], x_to,
+        )
+
+    def query_copy():
+        return remote(
+            packed_hbm.at[0, :, theirs], queries.at[x], query_s.at[0], query_r.at[0], x_to
+        )
+
+    def edge_copy(k, up, src, send):
+        where = {"dev": jnp.where(up, above, below)}
+        place = jnp.where(up, 0, 3)
+        return remote(
+            src, window.at[place, :, :, part_lanes(0, k)], send,
+            edge_r.at[jnp.where(up, 0, 1), k], where,
+        )
+
+    def early_copy(k):
+        return edge_copy(k, x == 1, packed_hbm.at[1:3, :, part_lanes(x, k)], early_s.at[k])
+
+    def late_copy(k):
+        return edge_copy(k, x == 0, window.at[2 - x, :, :, part_lanes(0, k)], late_s.at[k])
+
+    give_late = ((x == 0) & not_top) | ((x == 1) & not_bottom)
+    give_early = ((x == 1) & not_top) | ((x == 0) & not_bottom)
 
     def piece_rows(which, i):
         return pl.ds(pl.multiple_of(which * share + i * piece, SLOT), piece)
@@ -600,27 +614,37 @@
         return remote(block, block, wy_s.at[line, i], wy_r.at[line, i], y_to)
 
     for k in range(pairs):
-        near_copy(k).start()
-    for i in range(PIECES):
-
-        @pl.when(not_top)
-        def _():
-            wz_copy(z, i, 0, own_piece(i)).start()
-
-        @pl.when(not_bottom)
-        def _():
-            wz_copy(z, i, 1, own_piece(i)).start()
-
-    @pl.when(give_side)
+        pair_copy(k).start()
+    query_copy().start()
+
+    def send_pieces(pieces):
+        for i in pieces:
+
+            @pl.when(not_top)
+            def _():
+                wz_copy(z, i, 0, own_piece(i)).start()
+
+            @pl.when(not_bottom)
+            def _():
+                wz_copy(z, i, 1, own_piece(i)).start()
+
+    send_pieces(range(PIECES // 2))
+
+    @pl.when(give_early)
     def _():
-        for k in range(early, pairs):
-            way_copy(k).start()
-
+        for k in range(pairs):
+            early_copy(k).start()
+
+    send_pieces(range(PIECES // 2, PIECES))
     start_weights()
 
-    @pl.when(jnp.logical_not(have_far))
+    @pl.when(jnp.logical_not(not_bottom))
     def _():
-        near[x] = jnp.zeros_like(near[x])
+        window[0] = jnp.zeros_like(window[0])
+
+    @pl.when(jnp.logical_not(not_top))
+    def _():
+        window[3] = jnp.zeros_like(window[3])
 
     def way_of(line):
         return jnp.where(line < z, 0, 1)
@@ -651,50 +675,32 @@
             def _():
                 take(line, more(line), pieces)
 
+    for k in range(pairs):
+        pair_copy(k).wait_recv()
+
+        @pl.when(give_late)
+        def _():
+            late_copy(k).start()
+
     take_next(True, range(PIECES // 2))
     take_next(False, range(PIECES // 2))
-    for k in range(early):
-        near_copy(k).wait_recv()
-
-        @pl.when(give_far)
-        def _():
-            far_copy(k).start()
-
-    take_next(True, range(PIECES // 2, PIECES))
-    take_next(False, range(PIECES // 2, PIECES))
-
-    @pl.when(have_side)
-    def _():
-        for k in range(early, pairs):
-            way_copy(k).wait_recv()
-            side_copy(k).start()
-
-    for k in range(early, pairs):
-        near_copy(k).wait_recv()
-    for i in range(6):
+    for i in range(len(own_parts)):
         own_copy(i).wait()
+    query_copy().wait_recv()
 
     row = lax.broadcasted_iota(jnp.int32, (count, count), 0)
     col = lax.broadcasted_iota(jnp.int32, (count, count), 1)
-    see_before = (col >= row) & (me > 0)
-    see_after = (col <= row) & (me < devices - 1)
-
-    def mix_copy(k):
-        lanes = pl.ds(k * pair, pair)
-        return remote(
-            mixed.at[:, lanes], mixed_in.at[:, lanes], mix_s.at[k], mix_r.at[k], x_to
-        )
-
-    for k in range(pairs):
-
-        @pl.when(have_far)
-        def _():
-            far_copy(k).wait_recv()
-
-        for h in range(pair // HEAD):
-            lanes = slice(k * pair + h * HEAD, k * pair + (h + 1) * HEAD)
-            inner = slice(h * HEAD, (h + 1) * HEAD)
-            query = packed[0, :, lanes]
+
+    def mix_copy(b, k):
+        block = mixed.at[pl.ds(pl.multiple_of(b * count, count), count), part_lanes(x, k)]
+        return remote(block, block, mix_s.at[b, k], mix_r.at[b, k], x_to)
+
+    def attend(b, k):
+        see_before = (col >= row) & ((z > 0) | (b == 1))
+        see_after = (col <= row) & ((z < lines - 1) | (b == 0))
+        for h in range(PAIR // HEAD):
+            inner = slice(k * PAIR + h * HEAD, k * PAIR + (h + 1) * HEAD)
+            query = queries[b, :, inner]
 
             def score(keys):
                 return lax.dot_general(
@@ -703,23 +709,36 @@
 
             scores = jnp.concatenate(
                 [
-                    jnp.where(see_before, score(near[0, k, 0, :, inner]), NEG),
-                    score(packed[1, :, lanes]),
-                    jnp.where(see_after, score(near[1, k, 0, :, inner]), NEG),
+                    jnp.where(see_before, score(window[b, 0, :, inner]), NEG),
+                    score(window[b + 1, 0, :, inner]),
+                    jnp.where(see_after, score(window[b + 2, 0, :, inner]), NEG),
                 ],
                 axis=1,
             )
             top = jnp.max(scores, -1, keepdims=True)
             weight = jnp.exp(scores - top)
             weight = (weight / jnp.sum(weight, -1, keepdims=True)).astype(jnp.bfloat16)
-            values = jnp.concatenate(
-                [near[0, k, 1, :, inner], packed[2, :, lanes], near[1, k, 1, :, inner]], axis=0
+            values = jnp.concatenate([window[b + n, 1, :, inner] for n in range(3)], axis=0)
+            lanes = pl.ds(
+                pl.multiple_of(x * heads + k * PAIR + h * HEAD, HEAD), HEAD
             )
-            mixed[:, lanes] = jnp.dot(
+            mixed[pl.ds(pl.multiple_of(b * count, count), count), lanes] = jnp.dot(
                 weight, values, preferred_element_type=jnp.float32
             ).astype(jnp.bfloat16)
-        mix_copy(k).start()
-        if k + 1 == early:
+        mix_copy(b, k).start()
+
+    for b, up in ((1 - x, x == 1), (x, x == 0)):
+        for k in range(pairs):
+
+            @pl.when(jnp.where(up, not_bottom, not_top))
+            def _():
+                edge_copy(k, up, window.at[0, :, :, part_lanes(0, k)], early_s.at[k]).wait_recv()
+
+            attend(b, k)
+        if b is not x:
+            take_next(True, range(PIECES // 2, PIECES))
+            take_next(False, range(PIECES // 2, PIECES))
+        else:
             for line in near_lines:
 
                 @pl.when(distance(line) == 2)
@@ -729,12 +748,14 @@
     last = near_lines[-1]
     far_last = distance(last) > 2
 
-    @pl.when(far_last)
-    def _():
-        take(last, more(last))
-
-    for k in range(pairs):
-        mix_copy(k).wait_recv()
+    def take_last(pieces):
+        @pl.when(far_last)
+        def _():
+            take(last, more(last), pieces)
+
+    for b in range(COLS):
+        for k in range(pairs):
+            mix_copy(b, k).wait_recv()
 
     def place_of(which):
         return group if which == 0 else 1 - group
@@ -771,7 +792,9 @@
     def project(line, which, direct=False):
         place = place_of(which)
         block = column[line, pl.ds(pl.multiple_of(place * share, SLOT), share), :]
-        both = jnp.concatenate([mixed_in[...], mixed[...]], axis=0)
+        both = jnp.concatenate(
+            [mixed[pl.ds(pl.multiple_of(b * count, count), count), :] for b in (1 - x, x)], axis=0
+        )
         product = lax.dot_general(
             both, block, (((1,), (1,)), ((), ())), preferred_element_type=jnp.float32
         )
@@ -811,12 +834,13 @@
         return partial
 
     steps = [(line, which) for line in [z] + near_lines[:-1] for which in range(2)]
-    project(z, 0)
-    project(z, 1)
-    for line in near_lines[:-1]:
-        project(line, 0)
-        halves_in(line)
-        project(line, 1)
+    quarter = PIECES // 4
+    for i, (line, which) in enumerate(steps):
+        if which == 1 and i > 1:
+            halves_in(line)
+        project(line, which)
+        if i < 4:
+            take_last(range(i * quarter, (i + 1) * quarter))
     project(last, 0, True)
 
     @pl.when(jnp.logical_not(far_last))
@@ -854,24 +878,19 @@
     lifted = jnp.where(named, jax.nn.sigmoid(logits), 0.0)
     meta[...] = lifted / jnp.sum(lifted, 0, keepdims=True)
 
+    query_copy().wait_send()
     for k in range(pairs):
-        near_copy(k).wait_send()
-        mix_copy(k).wait_send()
-
-        if k < early:
-
-            @pl.when(give_far)
-            def _():
-                far_copy(k).wait_send()
-        else:
-
-            @pl.when(give_side)
-            def _():
-                way_copy(k).wait_send()
-
-            @pl.when(have_side)
-            def _():
-                side_copy(k).wait_send()
+        pair_copy(k).wait_send()
+        for b in range(COLS):
+            mix_copy(b, k).wait_send()
+
+        @pl.when(give_early)
+        def _():
+            early_copy(k).wait_send()
+
+        @pl.when(give_late)
+        def _():
+            late_copy(k).wait_send()
 
     for i in range(PIECES):
 
@@ -898,10 +917,10 @@
 
 def block_kernel(devices, *refs):
     sources, gate_up, down, out = refs[:6], refs[6], refs[7], refs[8]
-    held, normed, state, meta, wide = refs[9:14], refs[14], refs[15], refs[16], refs[17]
-    front_buffers, expert_buffers = refs[18:28], refs[28:44]
-    own_sem, gu_sem, dn_sem = refs[44:47]
-    front_sems, expert_sems = refs[47:66], refs[66:]
+    held, normed, state, meta, wide = refs[9:13], refs[13], refs[14], refs[15], refs[16]
+    front_buffers, expert_buffers = refs[17:26], refs[26:42]
+    own_sem, gu_sem, dn_sem = refs[42:45]
+    front_sems, expert_sems = refs[45:64], refs[64:]
     gu, dn = expert_buffers[5:7]
     squeeze, grow = expert_buffers[13:15]
     halves = gate_up.shape[0]
@@ -931,7 +950,7 @@
         *front_buffers, *front_sems,
     )
     expert_kernel(
-        devices, weight_copies, normed, meta, state, held[2], wide, out,
+        devices, weight_copies, normed, meta, state, held[1], wide, out,
         *expert_buffers, *expert_sems,
     )
 
@@ -964,16 +983,15 @@
         in_specs=[hbm] * 8,
         out_specs=pl.BlockSpec(memory_space=pltpu.VMEM),
         scratch_shapes=[
-            *[pltpu.VMEM(own[i].shape, own[i].dtype) for i in (0, 1, 3, 4, 5)],
+            *[pltpu.VMEM(own[i].shape, own[i].dtype) for i in (0, 3, 4, 5)],
             pltpu.VMEM((count, width), jnp.bfloat16),
             pltpu.VMEM((count, width), jnp.float32),
             pltpu.VMEM((router_weight.shape[1], count), jnp.float32),
             pltpu.VMEM((devices, slots + pack, half), jnp.bfloat16),
-            pltpu.VMEM((2, CHUNKS, 2, count, part), jnp.bfloat16),
-            pltpu.VMEM((CHUNKS // 2, 2, count, part), jnp.bfloat16),
+            pltpu.VMEM((4, 2, count, half // 2), jnp.bfloat16),
+            pltpu.VMEM((COLS, count, half // 2), jnp.bfloat16),
             pltpu.VMEM((lines, shard, half), jnp.bfloat16),
-            pltpu.VMEM((count, half), jnp.bfloat16),
-            pltpu.VMEM((count, half), jnp.bfloat16),
+            pltpu.VMEM((COLS * count, half), jnp.bfloat16),
             pltpu.VMEM((lines, 2, count, shard // 2), jnp.float32),
             pltpu.VMEM((lines, 2, count, shard // 2), jnp.float32),
             pltpu.VMEM((lines, 2, count, shard // 2), jnp.bfloat16),
@@ -995,11 +1013,12 @@
             pltpu.VMEM((pack, slots), jnp.bfloat16),
             pltpu.VMEM((slots, pack), jnp.bfloat16),
             pltpu.VMEM((count, part), jnp.float32),
-            dma((6,)), dma((halves,)), dma((halves,)),
-            dma((CHUNKS,)), dma((CHUNKS,)), dma((CHUNKS,)), dma((CHUNKS,)),
-            dma((CHUNKS // 2,)), dma((CHUNKS // 2,)), dma((CHUNKS // 2,)),
+            dma((7,)), dma((halves,)), dma((halves,)),
+            dma((half // 2 // PAIR,)), dma((half // 2 // PAIR,)), dma((1,)), dma((1,)),
+            dma((half // 2 // PAIR,)), dma((half // 2 // PAIR,)), dma((2, half // 2 // PAIR)),
             dma((lines, PIECES, 2)), dma((lines, PIECES)),
-            dma((lines, PIECES)), dma((lines, PIECES)), dma((CHUNKS,)), dma((CHUNKS,)),
+            dma((lines, PIECES)), dma((lines, PIECES)),
+            dma((COLS, half // 2 // PAIR)), dma((COLS, half // 2 // PAIR)),
             dma((lines, 2)), dma((lines, 2)), dma((lines, 2)), dma((lines, 2)),
             dma((lines, 2)), dma((lines, 2)),
             dma((lines,)), dma((lines,)),
@@ -1040,7 +1059,7 @@
     paired = parts == 2 and lax.axis_size("groups") == 2 and devices % COLS == 0
     experts_here = gate_up_weight.shape[0] // 2
     tiled = out_weight.shape[0] % (2 * LANES) == 0 and count == LANES
-    tiled = tiled and down_weight.shape[2] // CHUNKS % HEAD == 0 and devices == 4 * COLS
+    tiled = tiled and down_weight.shape[2] % (2 * PAIR) == 0 and devices == 4 * COLS
     tiled = tiled and down_weight.shape[2] % (2 * CHUNKS * LANES) == 0 and experts_here == devices
     tiled = tiled and SLOT * devices == LANES
     tiled = tiled and gate_up_weight.shape[3] % 64 == 0

time: 98.4 us -> 96.9 us (0.985)
  Pallas kernels: 96.6 us -> 95.1 us
    pallas_call x1, Pallas kernels: 96.6 us -> 95.1 us  [block_call(): pl.pallas_call(functools.partial(block_kernel, devices), out_shape=jax.Sh...]
where the time goes in v6:
time: 96.9 us; the launch traced here: 96.8 us
  Pallas kernels  95.1 us (98%)
  local copies, waits for them, and re-layouts  1.67 us (2%)
    pallas_call x1, Pallas kernels, block_call(): pl.pallas_call(functools.partial(block_kernel, devices), out_shape=jax.Sh...  95.1 us

profile of v6, /device:TPU:0, one launch (start us, length us, event | category | flops | bytes accessed | tf_op | source)
XLA Modules:
  0.0 96.8 jit_solution(5080400077165173754)
XLA Ops:
  0.0 95.1 %shard_map.82 = bf16[128,1024]{1,0:T(8,128)(2,1)} custom-call(bf16[128,2048]{1,0:T(8,128)(2,1)} %refs_0_.1, bf16[3,128,1024]{2,1,0:T(8,128)(2,1)} %bitcast.5, bf16[256,1024]{1,0:T(8,128)(2,1)} %refs_2_.1, f32[4,2048]{1,0:T(4,128)} %refs_3_.1, bf16[64,2048]{1,0:T(8,128)(2,1)} %bitcast.6, s32[4,128]{1,0:T(4,128)} %bitcast.7, ...), custom_call_target="tpu_custom_call" | custom-call | tf_op jit(solution)/shard_map/pallas_call | solution.py:980
  95.1 1.7 %copy.10 = bf16[128,1024]{1,0:T(8,128)(2,1)} copy(bf16[128,1024]{1,0:T(8,128)(2,1)} %shard_map.82) | data formatting | bytes 524288

commit v7 on v6

--- a/solution.py
+++ b/solution.py
@@ -70,6 +70,7 @@
 CHUNKS = 4
 PIECES = 4
 LAG = 2
+SPLIT = 2
 PAIR = 256
 VMEM_BYTES = 66 * 1000 * 1000
 MESH = pl.DeviceIdType.MESH
@@ -256,12 +257,12 @@
             left, right, (((1,), (1,)), ((), ())), preferred_element_type=jnp.float32
         )
 
-    def raise_side(e, side):
+    def raise_part(e, parts):
         sums = []
         for g in range(2):
             for b in range(2):
                 total = None
-                for c in range(chunks):
+                for side, c in parts:
                     start = side * half + c * wide_chunk
                     piece = across_rows(
                         gu[2 * e + b, g, :, start:start + wide_chunk], disp[side, c, e]
@@ -270,29 +271,32 @@
                 sums.append(total)
         return sums
 
-    def raise_first(e, carry):
-        for n, total in enumerate(raise_side(e, 1)):
-            raised[e, n * hidden:(n + 1) * hidden] = total
-        return carry
-
-    def raise_second(e, carry):
-        sums = [
-            total + raised[e, n * hidden:(n + 1) * hidden]
-            for n, total in enumerate(raise_side(e, 0))
-        ]
-        for b in range(2):
-            gate = sums[b]
-            hid_own[e, b * hidden:(b + 1) * hidden] = (
-                gate * jax.nn.sigmoid(gate) * sums[2 + b]
-            ).astype(jnp.bfloat16)
-        hid_copy(e).start()
-        return carry
+    def raise_some(parts, start, stop, first=False, last=False):
+        def one(e, carry):
+            sums = raise_part(e, parts)
+            if not first:
+                sums = [
+                    total + raised[e, n * hidden:(n + 1) * hidden] for n, total in enumerate(sums)
+                ]
+            if not last:
+                for n, total in enumerate(sums):
+                    raised[e, n * hidden:(n + 1) * hidden] = total
+                return carry
+            for b in range(2):
+                gate = sums[b]
+                hid_own[e, b * hidden:(b + 1) * hidden] = (
+                    gate * jax.nn.sigmoid(gate) * sums[2 + b]
+                ).astype(jnp.bfloat16)
+            hid_copy(e).start()
+            return carry
+
+        lax.fori_loop(start, stop, one, 0)
 
     def hid_copy(e):
         return remote(hid_own.at[e], hid_other.at[e], hid_s.at[e], hid_r.at[e], core_to)
 
-    def arrived():
-        for c in range(chunks):
+    def arrived(parts):
+        for c in parts:
             for s in range(devices):
                 core_copy(other, s, c).wait_recv()
 
@@ -309,9 +313,12 @@
 
     lax.fori_loop(0, 2 * local, weight_wait, 0)
 
+    offsets = [(jnp.abs(line - z) - 1) * chunks for line in near_lines]
+    offsets[1] = jnp.maximum(offsets[1], SPLIT)
+
     def step(t, carry):
-        for line in near_lines:
-            c = t - (jnp.abs(line - z) - 1) * chunks
+        for line, offset in zip(near_lines, offsets):
+            c = t - offset
 
             @pl.when((c >= 0) & (c < chunks))
             def _():
@@ -321,8 +328,8 @@
         def _():
             x_step(z, t - 1)
 
-        for line in near_lines:
-            c = t - LAG - (jnp.abs(line - z) - 1) * chunks
+        for line, offset in zip(near_lines, offsets):
+            c = t - LAG - offset
 
             @pl.when((c >= 0) & (c < chunks))
             def _():
@@ -332,27 +339,28 @@
 
     span = chunks * (lines - 1) + LAG
     lax.fori_loop(0, span - 2, step, 0)
-    first, second = local * 3 // 8, local * 5 // 8
-
-    def early_raise(start, stop):
-        @pl.when(part == 0)
-        def _():
-            if start == 0:
-                arrived()
-            lax.fori_loop(start, stop, raise_first, 0)
-
-    early_raise(0, first)
-    step(span - 2, 0)
-    early_raise(first, second)
-    step(span - 1, 0)
-    early_raise(second, local)
-
-    @pl.when(part == 1)
+    early = range(SPLIT)
+    late = range(SPLIT, chunks)
+    own_first = (part == 1) & ((z == 0) | (z == lines - 1))
+
+    @pl.when(own_first)
     def _():
-        lax.fori_loop(0, local, raise_first, 0)
-        arrived()
-
-    lax.fori_loop(0, local, raise_second, 0)
+        raise_some([(1, c) for c in early], 0, local, first=True)
+        step(span - 2, 0)
+        step(span - 1, 0)
+        raise_some([(1, c) for c in late], 0, local)
+        arrived(range(chunks))
+        raise_some([(0, c) for c in range(chunks)], 0, local, last=True)
+
+    @pl.when(jnp.logical_not(own_first))
+    def _():
+        arrived(early)
+        raise_some([(side, c) for c in early for side in range(2)], 0, local // 2, first=True)
+        step(span - 2, 0)
+        step(span - 1, 0)
+        raise_some([(side, c) for c in early for side in range(2)], local // 2, local, first=True)
+        arrived(late)
+        raise_some([(side, c) for c in late for side in range(2)], 0, local, last=True)
 
     group = 2 * wide_chunk
 
@@ -847,17 +855,21 @@
     def _():
         last_step()
 
-    for line, which in steps:
-        back_copy(line, which).wait_recv()
-        share_copy(line, which).start()
+    def relay(some):
+        for line, which in some:
+            back_copy(line, which).wait_recv()
+            share_copy(line, which).start()
+
+    relay(steps[:4])
+
+    @pl.when(far_last)
+    def _():
+        last_step()
+
+    relay(steps[4:])
     squares = jnp.zeros((count, share), jnp.float32)
     for line, which in steps:
         squares = squares + add_up(line, which)
-
-    @pl.when(far_last)
-    def _():
-        last_step()
-
     for which in range(2):
         back_copy(last, which).wait_recv()
         squares = squares + add_up(last, which)
@@ -878,41 +890,44 @@
     lifted = jnp.where(named, jax.nn.sigmoid(logits), 0.0)
     meta[...] = lifted / jnp.sum(lifted, 0, keepdims=True)
 
-    query_copy().wait_send()
-    for k in range(pairs):
-        pair_copy(k).wait_send()
-        for b in range(COLS):
-            mix_copy(b, k).wait_send()
-
-        @pl.when(give_early)
-        def _():
-            early_copy(k).wait_send()
-
-        @pl.when(give_late)
-        def _():
-            late_copy(k).wait_send()
-
-    for i in range(PIECES):
-
-        @pl.when(not_top)
-        def _():
-            wz_copy(z, i, 0, own_piece(i)).wait_send()
-
-        @pl.when(not_bottom)
-        def _():
-            wz_copy(z, i, 1, own_piece(i)).wait_send()
-
-        for line in near_lines:
-
-            @pl.when(more(line))
+    def drain():
+        query_copy().wait_send()
+        for k in range(pairs):
+            pair_copy(k).wait_send()
+            for b in range(COLS):
+                mix_copy(b, k).wait_send()
+
+            @pl.when(give_early)
             def _():
-                wz_copy(line, i, way_of(line)).wait_send()
-
-            wy_copy(line, i, group).wait_send()
-    for line, which in steps + [(last, 0), (last, 1)]:
-        sum_copy(line, which).wait_send()
-        back_copy(line, which).wait_send()
-        share_copy(line, which).wait_send()
+                early_copy(k).wait_send()
+
+            @pl.when(give_late)
+            def _():
+                late_copy(k).wait_send()
+
+        for i in range(PIECES):
+
+            @pl.when(not_top)
+            def _():
+                wz_copy(z, i, 0, own_piece(i)).wait_send()
+
+            @pl.when(not_bottom)
+            def _():
+                wz_copy(z, i, 1, own_piece(i)).wait_send()
+
+            for line in near_lines:
+
+                @pl.when(more(line))
+                def _():
+                    wz_copy(line, i, way_of(line)).wait_send()
+
+                wy_copy(line, i, group).wait_send()
+        for line, which in steps + [(last, 0), (last, 1)]:
+            sum_copy(line, which).wait_send()
+            back_copy(line, which).wait_send()
+            share_copy(line, which).wait_send()
+
+    return drain
 
 
 def block_kernel(devices, *refs):
@@ -945,7 +960,7 @@
             same = (packed == (slot - inner) // SLOT * CAP + inner) & (inner < CAP)
             ref[...] = jnp.where(same, 1.0, 0.0).astype(jnp.bfloat16)
 
-    front_kernel(
+    drain = front_kernel(
         devices, start_weights, sources, held, own_sem, normed, state, meta,
         *front_buffers, *front_sems,
     )
@@ -953,6 +968,7 @@
         devices, weight_copies, normed, meta, state, held[1], wide, out,
         *expert_buffers, *expert_sems,
     )
+    drain()
 
 
 def block_call(

time: 96.9 us -> 95.4 us (0.985)
  Pallas kernels: 95.1 us -> 93.6 us
    pallas_call x1, Pallas kernels: 95.1 us -> 93.6 us  [block_call(): pl.pallas_call(functools.partial(block_kernel, devices), out_shape=jax.Sh...]
where the time goes in v7:
time: 95.4 us; the launch traced here: 95.3 us
  Pallas kernels  93.6 us (98%)
  local copies, waits for them, and re-layouts  1.67 us (2%)
    pallas_call x1, Pallas kernels, block_call(): pl.pallas_call(functools.partial(block_kernel, devices), out_shape=jax.Sh...  93.6 us

profile of v7, /device:TPU:0, one launch (start us, length us, event | category | flops | bytes accessed | tf_op | source)
XLA Modules:
  0.0 95.3 jit_solution(700332762692729128)
XLA Ops:
  0.0 93.6 %shard_map.82 = bf16[128,1024]{1,0:T(8,128)(2,1)} custom-call(bf16[128,2048]{1,0:T(8,128)(2,1)} %refs_0_.1, bf16[3,128,1024]{2,1,0:T(8,128)(2,1)} %bitcast.5, bf16[256,1024]{1,0:T(8,128)(2,1)} %refs_2_.1, f32[4,2048]{1,0:T(4,128)} %refs_3_.1, bf16[64,2048]{1,0:T(8,128)(2,1)} %bitcast.6, s32[4,128]{1,0:T(4,128)} %bitcast.7, ...), custom_call_target="tpu_custom_call" | custom-call | tf_op jit(solution)/shard_map/pallas_call | solution.py:996
  93.6 1.7 %copy.10 = bf16[128,1024]{1,0:T(8,128)(2,1)} copy(bf16[128,1024]{1,0:T(8,128)(2,1)} %shard_map.82) | data formatting | bytes 524288

commit v8 on v7

--- a/solution.py
+++ b/solution.py
@@ -143,17 +143,17 @@
     def meta_copy(line):
         return remote(
             meta.at[pl.ds(pl.multiple_of(line * COLS * local, COLS * local), COLS * local)],
-            got_meta.at[z], meta_s.at[line], meta_r.at[z], {"dev": line * COLS + x},
+            got_meta.at[z], meta_s.at[0], meta_r.at[z], {"dev": line * COLS + x},
         )
 
     def meta_arrival(line):
-        return remote(got_meta.at[line], got_meta.at[line], meta_s.at[line], meta_r.at[line], x_to)
+        return remote(got_meta.at[line], got_meta.at[line], meta_s.at[0], meta_r.at[line], x_to)
 
     def z_copy(line, c, way, src=None):
         dst = tok.at[line, c]
         where = {"dev": jnp.where(way == 0, above, below)}
         return remote(
-            dst if src is None else src, dst, z_s.at[line, c, way], z_r.at[line, c], where
+            dst if src is None else src, dst, z_s.at[line, way], z_r.at[line, c], where
         )
 
     def packed_out(line, c):
@@ -161,12 +161,12 @@
 
     def x_copy(line, c):
         return remote(
-            packed_out(line, c), got_packed.at[line, c], x_s.at[line, c], x_r.at[line, c], x_to
+            packed_out(line, c), got_packed.at[line, c], x_s.at[0], x_r.at[line, c], x_to
         )
 
     def core_copy(which, s, c):
         place = disp.at[which, c, :, slot_rows(s), :]
-        return remote(place, place, core_s.at[s, c], core_r.at[s, c], core_to)
+        return remote(place, place, core_s.at[0], core_r.at[jnp.where(c < SPLIT, 0, 1)], core_to)
 
     def own_send(c):
         src = normed.at[:, own_lanes(c)]
@@ -293,12 +293,15 @@
         lax.fori_loop(start, stop, one, 0)
 
     def hid_copy(e):
-        return remote(hid_own.at[e], hid_other.at[e], hid_s.at[e], hid_r.at[e], core_to)
-
-    def arrived(parts):
-        for c in parts:
-            for s in range(devices):
-                core_copy(other, s, c).wait_recv()
+        return remote(hid_own.at[e], hid_other.at[e], hid_s.at[0], hid_r.at[e], core_to)
+
+    def arrived(which):
+        span_of = pl.ds(which * SPLIT, SPLIT) if which == 0 else pl.ds(SPLIT, chunks - SPLIT)
+        block = disp.at[other, span_of]
+        remote(block, block, core_s.at[0], core_r.at[which], core_to).wait_recv()
+
+    def sent(ref, sem):
+        remote(ref, ref, sem, sem, core_to).wait_send()
 
     routing(
         z, meta[expert_rows(z * COLS * local, x)], meta[expert_rows(z * COLS * local, 1 - x)]
@@ -306,12 +309,8 @@
     for c in range(chunks):
         own_step(c)
 
-    def weight_wait(h, carry):
-        for copy in weight_copies(h):
-            copy.wait()
-        return carry
-
-    lax.fori_loop(0, 2 * local, weight_wait, 0)
+    for copy in weight_copies():
+        copy.wait()
 
     offsets = [(jnp.abs(line - z) - 1) * chunks for line in near_lines]
     offsets[1] = jnp.maximum(offsets[1], SPLIT)
@@ -349,17 +348,18 @@
         step(span - 2, 0)
         step(span - 1, 0)
         raise_some([(1, c) for c in late], 0, local)
-        arrived(range(chunks))
+        arrived(0)
+        arrived(1)
         raise_some([(0, c) for c in range(chunks)], 0, local, last=True)
 
     @pl.when(jnp.logical_not(own_first))
     def _():
-        arrived(early)
+        arrived(0)
         raise_some([(side, c) for c in early for side in range(2)], 0, local // 2, first=True)
         step(span - 2, 0)
         step(span - 1, 0)
         raise_some([(side, c) for c in early for side in range(2)], local // 2, local, first=True)
-        arrived(late)
+        arrived(1)
         raise_some([(side, c) for c in late for side in range(2)], 0, local, last=True)
 
     group = 2 * wide_chunk
@@ -390,14 +390,14 @@
     def rx_copy(line, q):
         return remote(
             wide.at[lines + line, pl.ds(slots, pack), lanes_of(q)], got_rows.at[line, q],
-            rx_s.at[line, q], rx_r.at[line, q], x_to,
+            rx_s.at[0], rx_r.at[line, q], x_to,
         )
 
     def rz_copy(line, q, way):
         where = {"dev": jnp.where(way == 0, above, below)}
         return remote(
             tok.at[line, q], got_sum.at[way, line, q],
-            rz_s.at[line, q], rz_r.at[way, line, q], where,
+            rz_s.at[0], rz_r.at[way, line, q], where,
         )
 
     def give(line, q):
@@ -441,8 +441,7 @@
 
         @pl.when(jnp.where(low, not_top, not_bottom))
         def _():
-            for c in range(chunks):
-                z_copy(line, c, jnp.where(low, 0, 1)).wait_send()
+            sent(tok.at[line], z_s.at[line, jnp.where(low, 0, 1)])
 
     far_end = (z == 0) | (z == lines - 1)
 
@@ -485,31 +484,20 @@
             state[:, own] + (1.0 + modulation[3:4, own]) * acc[...]
         ).astype(out.dtype)
 
-    for c in range(chunks):
-
-        @pl.when(not_top)
-        def _():
-            z_copy(z, c, 0, normed.at[:, own_lanes(c)]).wait_send()
-
-        @pl.when(not_bottom)
-        def _():
-            z_copy(z, c, 1, normed.at[:, own_lanes(c)]).wait_send()
-
-        for line in near_lines:
-            rz_copy(line, c, jnp.where(line > z, 0, 1)).wait_send()
-        for line in range(lines):
-            x_copy(line, c).wait_send()
-            rx_copy(line, c).wait_send()
-        for s in range(devices):
-            core_copy(part, s, c).wait_send()
-    for line in near_lines:
-        meta_copy(line).wait_send()
-
-    def hid_drain(e, carry):
-        hid_copy(e).wait_send()
-        return carry
-
-    lax.fori_loop(0, local, hid_drain, 0)
+    @pl.when(not_top)
+    def _():
+        sent(tok.at[z], z_s.at[z, 0])
+
+    @pl.when(not_bottom)
+    def _():
+        sent(tok.at[z], z_s.at[z, 1])
+
+    sent(tok.at[pl.ds(0, lines - 1)], rz_s.at[0])
+    sent(got_packed, x_s.at[0])
+    sent(got_rows, rx_s.at[0])
+    sent(disp.at[part], core_s.at[0])
+    sent(got_meta.at[pl.ds(0, lines - 1)], meta_s.at[0])
+    sent(hid_own, hid_s.at[0])
 
 
 def front_kernel(
@@ -611,7 +599,7 @@
         dst = column.at[line, piece_rows(group, i)]
         where = {"dev": jnp.where(way == 0, above, below)}
         return remote(
-            dst if src is None else src, dst, wz_s.at[line, i, way], wz_r.at[line, i], where
+            dst if src is None else src, dst, wz_s.at[line, way], wz_r.at[line, i], where
         )
 
     def own_piece(i):
@@ -619,7 +607,7 @@
 
     def wy_copy(line, i, which):
         block = column.at[line, piece_rows(which, i)]
-        return remote(block, block, wy_s.at[line, i], wy_r.at[line, i], y_to)
+        return remote(block, block, wy_s.at[0], wy_r.at[line], y_to)
 
     for k in range(pairs):
         pair_copy(k).start()
@@ -701,7 +689,7 @@
 
     def mix_copy(b, k):
         block = mixed.at[pl.ds(pl.multiple_of(b * count, count), count), part_lanes(x, k)]
-        return remote(block, block, mix_s.at[b, k], mix_r.at[b, k], x_to)
+        return remote(block, block, mix_s.at[0], mix_r.at[0], x_to)
 
     def attend(b, k):
         see_before = (col >= row) & ((z > 0) | (b == 1))
@@ -761,9 +749,8 @@
         def _():
             take(last, more(last), pieces)
 
-    for b in range(COLS):
-        for k in range(pairs):
-            mix_copy(b, k).wait_recv()
+    mix_block = mixed.at[:, theirs]
+    remote(mix_block, mix_block, mix_s.at[0], mix_r.at[0], x_to).wait_recv()
 
     def place_of(which):
         return group if which == 0 else 1 - group
@@ -772,28 +759,28 @@
         place = place_of(which)
         return remote(
             mine_out.at[line, place], their_out.at[line, place],
-            sum_s.at[line, which], sum_r.at[line, which], core_to,
+            sum_s.at[0], sum_r.at[line, which], core_to,
         )
 
     def back_copy(line, which):
         place = place_of(which)
         return remote(
             sent_back.at[line, place], got_back.at[line, place],
-            back_s.at[line, which], back_r.at[line, which], x_to,
+            back_s.at[0], back_r.at[line, which], x_to,
         )
 
     def share_copy(line, which):
         place = place_of(which)
         return remote(
             got_back.at[line, place], their_back.at[line, place],
-            share_s.at[line, which], share_r.at[line, which], core_to,
+            share_s.at[0], share_r.at[line, which], core_to,
         )
 
     def direct_copy(which):
         place = place_of(which)
         return remote(
             sent_back.at[last, place], their_back.at[last, place],
-            share_s.at[last, which], share_r.at[last, which],
+            share_s.at[0], share_r.at[last, which],
             {"dev": z * COLS + (1 - x), "sub": 1 - part},
         )
 
@@ -814,8 +801,8 @@
         sum_copy(line, which).start()
 
     def halves_in(line):
-        for n in range(PIECES):
-            wy_copy(line, n, 1 - group).wait_recv()
+        block = column.at[line, pl.ds(pl.multiple_of((1 - group) * share, SLOT), share)]
+        remote(block, block, wy_s.at[0], wy_r.at[line], y_to).wait_recv()
 
     def last_step():
         halves_in(last)
@@ -891,11 +878,13 @@
     meta[...] = lifted / jnp.sum(lifted, 0, keepdims=True)
 
     def drain():
+        def sent(ref, sem):
+            remote(ref, ref, sem, sem, x_to).wait_send()
+
         query_copy().wait_send()
+        sent(mixed.at[:, ours], mix_s.at[0])
         for k in range(pairs):
             pair_copy(k).wait_send()
-            for b in range(COLS):
-                mix_copy(b, k).wait_send()
 
             @pl.when(give_early)
             def _():
@@ -905,27 +894,26 @@
             def _():
                 late_copy(k).wait_send()
 
-        for i in range(PIECES):
-
-            @pl.when(not_top)
+        half_shard = column.at[0, pl.ds(0, share)]
+
+        @pl.when(not_top)
+        def _():
+            sent(half_shard, wz_s.at[z, 0])
+
+        @pl.when(not_bottom)
+        def _():
+            sent(half_shard, wz_s.at[z, 1])
+
+        for line in near_lines:
+
+            @pl.when(more(line))
             def _():
-                wz_copy(z, i, 0, own_piece(i)).wait_send()
-
-            @pl.when(not_bottom)
-            def _():
-                wz_copy(z, i, 1, own_piece(i)).wait_send()
-
-            for line in near_lines:
-
-                @pl.when(more(line))
-                def _():
-                    wz_copy(line, i, way_of(line)).wait_send()
-
-                wy_copy(line, i, group).wait_send()
-        for line, which in steps + [(last, 0), (last, 1)]:
-            sum_copy(line, which).wait_send()
-            back_copy(line, which).wait_send()
-            share_copy(line, which).wait_send()
+                sent(half_shard, wz_s.at[line, way_of(line)])
+
+        sent(column.at[pl.ds(0, lines - 1), pl.ds(0, share)], wy_s.at[0])
+        sent(mine_out, sum_s.at[0])
+        sent(sent_back, back_s.at[0])
+        sent(got_back, share_s.at[0])
 
     return drain
 
@@ -938,21 +926,15 @@
     front_sems, expert_sems = refs[45:64], refs[64:]
     gu, dn = expert_buffers[5:7]
     squeeze, grow = expert_buffers[13:15]
-    halves = gate_up.shape[0]
-
-    def weight_copies(h):
+    def weight_copies():
         return (
-            pltpu.make_async_copy(gate_up.at[h], gu.at[h], gu_sem.at[h]),
-            pltpu.make_async_copy(down.at[h], dn.at[h], dn_sem.at[h]),
+            pltpu.make_async_copy(gate_up, gu, gu_sem.at[0]),
+            pltpu.make_async_copy(down, dn, dn_sem.at[0]),
         )
 
     def start_weights():
-        def one(h, carry):
-            for copy in weight_copies(h):
-                copy.start()
-            return carry
-
-        lax.fori_loop(0, halves, one, 0)
+        for copy in weight_copies():
+            copy.start()
         for ref, axis in ((squeeze, 0), (grow, 1)):
             packed = lax.broadcasted_iota(jnp.int32, ref.shape, axis)
             slot = lax.broadcasted_iota(jnp.int32, ref.shape, 1 - axis)
@@ -986,6 +968,7 @@
     rows = devices * SLOT
     slots, pack = local * SLOT, local * CAP
     part = half // CHUNKS
+    pairs = half // 2 // PAIR
     shard = out_weight.shape[0]
     own = (
         tokens, query_key_value.transpose(1, 0, 2), out_weight, modulation,
@@ -1029,21 +1012,15 @@
             pltpu.VMEM((pack, slots), jnp.bfloat16),
             pltpu.VMEM((slots, pack), jnp.bfloat16),
             pltpu.VMEM((count, part), jnp.float32),
-            dma((7,)), dma((halves,)), dma((halves,)),
-            dma((half // 2 // PAIR,)), dma((half // 2 // PAIR,)), dma((1,)), dma((1,)),
-            dma((half // 2 // PAIR,)), dma((half // 2 // PAIR,)), dma((2, half // 2 // PAIR)),
-            dma((lines, PIECES, 2)), dma((lines, PIECES)),
-            dma((lines, PIECES)), dma((lines, PIECES)),
-            dma((COLS, half // 2 // PAIR)), dma((COLS, half // 2 // PAIR)),
-            dma((lines, 2)), dma((lines, 2)), dma((lines, 2)), dma((lines, 2)),
-            dma((lines, 2)), dma((lines, 2)),
-            dma((lines,)), dma((lines,)),
-            dma((lines, CHUNKS, 2)), dma((lines, CHUNKS)),
-            dma((lines, CHUNKS)), dma((lines, CHUNKS)),
-            dma((devices, CHUNKS)), dma((devices, CHUNKS)),
-            dma((local,)), dma((local,)),
-            dma((lines, CHUNKS)), dma((lines, CHUNKS)),
-            dma((lines, CHUNKS)), dma((2, lines, CHUNKS)),
+            dma((7,)), dma((1,)), dma((1,)),
+            dma((pairs,)), dma((pairs,)), dma((1,)), dma((1,)),
+            dma((pairs,)), dma((pairs,)), dma((2, pairs)),
+            dma((lines, 2)), dma((lines, PIECES)), dma((1,)), dma((lines,)), dma((1,)), dma((1,)),
+            dma((1,)), dma((lines, 2)), dma((1,)), dma((lines, 2)), dma((1,)), dma((lines, 2)),
+            dma((1,)), dma((lines,)),
+            dma((lines, 2)), dma((lines, CHUNKS)), dma((1,)), dma((lines, CHUNKS)),
+            dma((1,)), dma((2,)), dma((1,)), dma((local,)),
+            dma((1,)), dma((lines, CHUNKS)), dma((1,)), dma((2, lines, CHUNKS)),
         ],
         compiler_params=pltpu.CompilerParams(
             collective_id=1, has_side_effects=True, vmem_limit_bytes=VMEM_BYTES

time: 95.4 us -> 93 us (0.975)
  Pallas kernels: 93.6 us -> 91.2 us
    pallas_call x1, Pallas kernels: 93.6 us -> 91.2 us  [block_call(): pl.pallas_call(functools.partial(block_kernel, devices), out_shape=jax.Sh...]
where the time goes in v8:
time: 93 us; the launch traced here: 92.9 us
  Pallas kernels  91.2 us (98%)
  local copies, waits for them, and re-layouts  1.67 us (2%)
    pallas_call x1, Pallas kernels, block_call(): pl.pallas_call(functools.partial(block_kernel, devices), out_shape=jax.Sh...  91.2 us

profile of v8, /device:TPU:0, one launch (start us, length us, event | category | flops | bytes accessed | tf_op | source)
XLA Modules:
  0.0 92.9 jit_solution(9312610447690471307)
XLA Ops:
  0.0 91.2 %shard_map.82 = bf16[128,1024]{1,0:T(8,128)(2,1)} custom-call(bf16[128,2048]{1,0:T(8,128)(2,1)} %refs_0_.1, bf16[3,128,1024]{2,1,0:T(8,128)(2,1)} %bitcast.5, bf16[256,1024]{1,0:T(8,128)(2,1)} %refs_2_.1, f32[4,2048]{1,0:T(4,128)} %refs_3_.1, bf16[64,2048]{1,0:T(8,128)(2,1)} %bitcast.6, s32[4,128]{1,0:T(4,128)} %bitcast.7, ...), custom_call_target="tpu_custom_call" | custom-call | tf_op jit(solution)/shard_map/pallas_call | solution.py:979
  91.2 1.7 %copy.10 = bf16[128,1024]{1,0:T(8,128)(2,1)} copy(bf16[128,1024]{1,0:T(8,128)(2,1)} %shard_map.82) | data formatting | bytes 524288

commit v9 on v8

--- a/solution.py
+++ b/solution.py
@@ -69,7 +69,7 @@
 COLS = 2
 CHUNKS = 4
 PIECES = 4
-LAG = 2
+LAG = 4
 SPLIT = 2
 PAIR = 256
 VMEM_BYTES = 66 * 1000 * 1000
@@ -293,7 +293,7 @@
         lax.fori_loop(start, stop, one, 0)
 
     def hid_copy(e):
-        return remote(hid_own.at[e], hid_other.at[e], hid_s.at[0], hid_r.at[e], core_to)
+        return remote(hid_own.at[e], hid_other.at[e], hid_s.at[0], hid_r.at[e // (local // 2)], core_to)
 
     def arrived(which):
         span_of = pl.ds(which * SPLIT, SPLIT) if which == 0 else pl.ds(SPLIT, chunks - SPLIT)
@@ -323,9 +323,9 @@
             def _():
                 line_step(line, c)
 
-        @pl.when((t >= 1) & (t < 1 + chunks))
-        def _():
-            x_step(z, t - 1)
+        @pl.when((t >= LAG - 1) & (t < LAG - 1 + chunks))
+        def _():
+            x_step(z, t - LAG + 1)
 
         for line, offset in zip(near_lines, offsets):
             c = t - LAG - offset
@@ -368,8 +368,6 @@
         lanes = slice(g * group, (g + 1) * group)
 
         def one(e, carry):
-            if g == 0:
-                hid_copy(e).wait_recv()
             mine = pl.ds(pl.multiple_of(part * hidden, SLOT), hidden)
             theirs = pl.ds(pl.multiple_of(other * hidden, SLOT), hidden)
             left = jnp.concatenate([hid_own[e], hid_other[e]], axis=0)
@@ -382,7 +380,11 @@
             ).astype(jnp.bfloat16)
             return carry
 
-        lax.fori_loop(0, local, one, 0)
+        for which in range(2):
+            if g == 0:
+                block = hid_other.at[pl.ds(which * (local // 2), local // 2)]
+                remote(block, block, hid_s.at[0], hid_r.at[which], core_to).wait_recv()
+            lax.fori_loop(which * (local // 2), (which + 1) * (local // 2), one, 0)
 
     def result_rows(s, q):
         return wide[:local, slot_rows(s), lanes_of(q)].reshape(slots, wide_chunk)
@@ -393,11 +395,12 @@
             rx_s.at[0], rx_r.at[line, q], x_to,
         )
 
-    def rz_copy(line, q, way):
+    def rz_copy(line, q, way, owner=None):
+        owner = z - 1 if owner is None else owner
         where = {"dev": jnp.where(way == 0, above, below)}
         return remote(
             tok.at[line, q], got_sum.at[way, line, q],
-            rz_s.at[0], rz_r.at[way, line, q], where,
+            rz_s.at[0], rz_r.at[jnp.where((way == 1) & (line == owner), lines, line), q], where,
         )
 
     def give(line, q):
@@ -415,7 +418,7 @@
         )
 
     def add_line(line, q, way):
-        rz_copy(line, q, way).wait_recv()
+        rz_copy(line, q, way, z).wait_recv()
         acc[...] += got_sum[way, line, q].astype(jnp.float32)
 
     def pass_on(line, q):
@@ -755,32 +758,38 @@
     def place_of(which):
         return group if which == 0 else 1 - group
 
+    def group_of(line):
+        return jnp.where(line == last, 1, 0)
+
+    def come(ref, sem):
+        remote(ref, ref, sum_s.at[0], sem, core_to).wait_recv()
+
     def sum_copy(line, which):
         place = place_of(which)
         return remote(
             mine_out.at[line, place], their_out.at[line, place],
-            sum_s.at[0], sum_r.at[line, which], core_to,
+            sum_s.at[0], sum_r.at[group_of(line)], core_to,
         )
 
     def back_copy(line, which):
         place = place_of(which)
         return remote(
             sent_back.at[line, place], got_back.at[line, place],
-            back_s.at[0], back_r.at[line, which], x_to,
+            back_s.at[0], back_r.at[line], x_to,
         )
 
     def share_copy(line, which):
         place = place_of(which)
         return remote(
             got_back.at[line, place], their_back.at[line, place],
-            share_s.at[0], share_r.at[line, which], core_to,
+            share_s.at[0], share_r.at[group_of(line)], core_to,
         )
 
     def direct_copy(which):
         place = place_of(which)
         return remote(
             sent_back.at[last, place], their_back.at[last, place],
-            share_s.at[0], share_r.at[last, which],
+            share_s.at[0], share_r.at[1],
             {"dev": z * COLS + (1 - x), "sub": 1 - part},
         )
 
@@ -810,8 +819,6 @@
 
     def add_up(line, which):
         place = place_of(which)
-        sum_copy(line, which).wait_recv()
-        share_copy(line, which).wait_recv()
         partial = jnp.zeros((count, share), jnp.float32)
         for column_of, total in (
             (x, mine_out[line, place] + their_out[line, place]),
@@ -844,7 +851,8 @@
 
     def relay(some):
         for line, which in some:
-            back_copy(line, which).wait_recv()
+            if which == 0:
+                come(got_back.at[line], back_r.at[line])
             share_copy(line, which).start()
 
     relay(steps[:4])
@@ -855,10 +863,14 @@
 
     relay(steps[4:])
     squares = jnp.zeros((count, share), jnp.float32)
+    come(mine_out.at[pl.ds(0, lines - 1)], sum_r.at[0])
+    come(got_back.at[pl.ds(0, lines - 1)], share_r.at[0])
     for line, which in steps:
         squares = squares + add_up(line, which)
+    come(got_back.at[last], back_r.at[last])
+    come(mine_out.at[last], sum_r.at[1])
+    come(got_back.at[last], share_r.at[1])
     for which in range(2):
-        back_copy(last, which).wait_recv()
         squares = squares + add_up(last, which)
     square = jnp.sum(squares, -1, keepdims=True)
     scale = lax.rsqrt(square / width + EPS)
@@ -1016,11 +1028,11 @@
             dma((pairs,)), dma((pairs,)), dma((1,)), dma((1,)),
             dma((pairs,)), dma((pairs,)), dma((2, pairs)),
             dma((lines, 2)), dma((lines, PIECES)), dma((1,)), dma((lines,)), dma((1,)), dma((1,)),
-            dma((1,)), dma((lines, 2)), dma((1,)), dma((lines, 2)), dma((1,)), dma((lines, 2)),
+            dma((1,)), dma((2,)), dma((1,)), dma((lines,)), dma((1,)), dma((2,)),
             dma((1,)), dma((lines,)),
             dma((lines, 2)), dma((lines, CHUNKS)), dma((1,)), dma((lines, CHUNKS)),
-            dma((1,)), dma((2,)), dma((1,)), dma((local,)),
-            dma((1,)), dma((lines, CHUNKS)), dma((1,)), dma((2, lines, CHUNKS)),
+            dma((1,)), dma((2,)), dma((1,)), dma((2,)),
+            dma((1,)), dma((lines, CHUNKS)), dma((1,)), dma((lines + 1, CHUNKS)),
         ],
         compiler_params=pltpu.CompilerParams(
             collective_id=1, has_side_effects=True, vmem_limit_bytes=VMEM_BYTES

time: 93 us -> 92.6 us (level)
  no operation moved by 1% of the time
where the time goes in v9:
time: 92.6 us; the launch traced here: 92.4 us
  Pallas kernels  90.8 us (98%)
  local copies, waits for them, and re-layouts  1.67 us (2%)
    pallas_call x1, Pallas kernels, block_call(): pl.pallas_call(functools.partial(block_kernel, devices), out_shape=jax.Sh...  90.8 us

profile of v9, /device:TPU:0, one launch (start us, length us, event | category | flops | bytes accessed | tf_op | source)
XLA Modules:
  0.0 92.4 jit_solution(2659719971095746690)
XLA Ops:
  0.0 90.8 %shard_map.82 = bf16[128,1024]{1,0:T(8,128)(2,1)} custom-call(bf16[128,2048]{1,0:T(8,128)(2,1)} %refs_0_.1, bf16[3,128,1024]{2,1,0:T(8,128)(2,1)} %bitcast.5, bf16[256,1024]{1,0:T(8,128)(2,1)} %refs_2_.1, f32[4,2048]{1,0:T(4,128)} %refs_3_.1, bf16[64,2048]{1,0:T(8,128)(2,1)} %bitcast.6, s32[4,128]{1,0:T(4,128)} %bitcast.7, ...), custom_call_target="tpu_custom_call" | custom-call | tf_op jit(solution)/shard_map/pallas_call | solution.py:991
  90.8 1.7 %copy.10 = bf16[128,1024]{1,0:T(8,128)(2,1)} copy(bf16[128,1024]{1,0:T(8,128)(2,1)} %shard_map.82) | data formatting | bytes 524288

commit v10 on v9

--- a/solution.py
+++ b/solution.py
@@ -153,7 +153,7 @@
         dst = tok.at[line, c]
         where = {"dev": jnp.where(way == 0, above, below)}
         return remote(
-            dst if src is None else src, dst, z_s.at[line, way], z_r.at[line, c], where
+            dst if src is None else src, dst, z_s.at[jnp.where((line == z) & (way == 1), lines, line)], z_r.at[line, c], where
         )
 
     def packed_out(line, c):
@@ -161,7 +161,7 @@
 
     def x_copy(line, c):
         return remote(
-            packed_out(line, c), got_packed.at[line, c], x_s.at[0], x_r.at[line, c], x_to
+            packed_out(line, c), got_packed.at[line, c], x_s.at[0], x_r.at[line, c // 2], x_to
         )
 
     def core_copy(which, s, c):
@@ -245,7 +245,11 @@
         spread(line, c, tok[line, c])
 
     def x_step(line, c):
-        x_copy(line, c).wait_recv()
+        @pl.when(c % 2 == 0)
+        def _():
+            block = got_packed.at[line, pl.ds(c, 2)]
+            remote(block, block, x_s.at[0], x_r.at[line, c // 2], x_to).wait_recv()
+
         s = line * COLS + (1 - x)
         disp[part, c, :, slot_rows(s), :] = jnp.dot(
             grow[...], got_packed[line, c], preferred_element_type=jnp.float32
@@ -364,7 +368,7 @@
 
     group = 2 * wide_chunk
 
-    def lower(g):
+    def lower(g, between):
         lanes = slice(g * group, (g + 1) * group)
 
         def one(e, carry):
@@ -385,6 +389,8 @@
                 block = hid_other.at[pl.ds(which * (local // 2), local // 2)]
                 remote(block, block, hid_s.at[0], hid_r.at[which], core_to).wait_recv()
             lax.fori_loop(which * (local // 2), (which + 1) * (local // 2), one, 0)
+            if which == 0:
+                between()
 
     def result_rows(s, q):
         return wide[:local, slot_rows(s), lanes_of(q)].reshape(slots, wide_chunk)
@@ -432,10 +438,11 @@
         tok[line, q] = acc[...].astype(jnp.bfloat16)
         rz_copy(line, q, way).start()
 
-    for g in range(half // group):
-        lower(g)
-        for q in range(2 * g, 2 * g + 2):
-            give(far_lines[0], q)
+    lower(0, lambda: None)
+    give(far_lines[0], 0)
+    lower(1, lambda: give(far_lines[0], 1))
+    for q in range(2, chunks):
+        give(far_lines[0], q)
     def give_all(line):
         lax.fori_loop(0, chunks, lambda q, carry: (give(line, q), carry)[1], 0)
 
@@ -444,7 +451,7 @@
 
         @pl.when(jnp.where(low, not_top, not_bottom))
         def _():
-            sent(tok.at[line], z_s.at[line, jnp.where(low, 0, 1)])
+            sent(tok.at[line], z_s.at[line])
 
     far_end = (z == 0) | (z == lines - 1)
 
@@ -489,11 +496,11 @@
 
     @pl.when(not_top)
     def _():
-        sent(tok.at[z], z_s.at[z, 0])
+        sent(tok.at[z], z_s.at[z])
 
     @pl.when(not_bottom)
     def _():
-        sent(tok.at[z], z_s.at[z, 1])
+        sent(tok.at[z], z_s.at[lines])
 
     sent(tok.at[pl.ds(0, lines - 1)], rz_s.at[0])
     sent(got_packed, x_s.at[0])
@@ -602,7 +609,8 @@
         dst = column.at[line, piece_rows(group, i)]
         where = {"dev": jnp.where(way == 0, above, below)}
         return remote(
-            dst if src is None else src, dst, wz_s.at[line, way], wz_r.at[line, i], where
+            dst if src is None else src, dst,
+            wz_s.at[jnp.where((line == z) & (way == 1), lines, line)], wz_r.at[line, i], where
         )
 
     def own_piece(i):
@@ -910,17 +918,17 @@
 
         @pl.when(not_top)
         def _():
-            sent(half_shard, wz_s.at[z, 0])
+            sent(half_shard, wz_s.at[z])
 
         @pl.when(not_bottom)
         def _():
-            sent(half_shard, wz_s.at[z, 1])
+            sent(half_shard, wz_s.at[lines])
 
         for line in near_lines:
 
             @pl.when(more(line))
             def _():
-                sent(half_shard, wz_s.at[line, way_of(line)])
+                sent(half_shard, wz_s.at[line])
 
         sent(column.at[pl.ds(0, lines - 1), pl.ds(0, share)], wy_s.at[0])
         sent(mine_out, sum_s.at[0])
@@ -1027,10 +1035,10 @@
             dma((7,)), dma((1,)), dma((1,)),
             dma((pairs,)), dma((pairs,)), dma((1,)), dma((1,)),
             dma((pairs,)), dma((pairs,)), dma((2, pairs)),
-            dma((lines, 2)), dma((lines, PIECES)), dma((1,)), dma((lines,)), dma((1,)), dma((1,)),
+            dma((lines + 1,)), dma((lines, PIECES)), dma((1,)), dma((lines,)), dma((1,)), dma((1,)),
             dma((1,)), dma((2,)), dma((1,)), dma((lines,)), dma((1,)), dma((2,)),
             dma((1,)), dma((lines,)),
-            dma((lines, 2)), dma((lines, CHUNKS)), dma((1,)), dma((lines, CHUNKS)),
+            dma((lines + 1,)), dma((lines, CHUNKS)), dma((1,)), dma((lines, CHUNKS // 2)),
             dma((1,)), dma((2,)), dma((1,)), dma((2,)),
             dma((1,)), dma((lines, CHUNKS)), dma((1,)), dma((lines + 1, CHUNKS)),
         ],
@@ -1064,7 +1072,7 @@
     paired = parts == 2 and lax.axis_size("groups") == 2 and devices % COLS == 0
     experts_here = gate_up_weight.shape[0] // 2
     tiled = out_weight.shape[0] % (2 * LANES) == 0 and count == LANES
-    tiled = tiled and down_weight.shape[2] % (2 * PAIR) == 0 and devices == 4 * COLS
+    tiled = tiled and down_weight.shape[2] == 4 * PAIR and devices == 4 * COLS
     tiled = tiled and down_weight.shape[2] % (2 * CHUNKS * LANES) == 0 and experts_here == devices
     tiled = tiled and SLOT * devices == LANES
     tiled = tiled and gate_up_weight.shape[3] % 64 == 0

time: 92.6 us -> 92.5 us (level)
  no operation moved by 1% of the time
where the time goes in v10:
time: 92.5 us; the launch traced here: 92.4 us
  Pallas kernels  90.7 us (98%)
  local copies, waits for them, and re-layouts  1.67 us (2%)
    pallas_call x1, Pallas kernels, block_call(): pl.pallas_call(functools.partial(block_kernel, devices), out_shape=jax.Sh...  90.7 us

profile of v10, /device:TPU:0, one launch (start us, length us, event | category | flops | bytes accessed | tf_op | source)
XLA Modules:
  0.0 92.4 jit_solution(12889293301988580892)
XLA Ops:
  0.0 90.7 %shard_map.82 = bf16[128,1024]{1,0:T(8,128)(2,1)} custom-call(bf16[128,2048]{1,0:T(8,128)(2,1)} %refs_0_.1, bf16[3,128,1024]{2,1,0:T(8,128)(2,1)} %bitcast.5, bf16[256,1024]{1,0:T(8,128)(2,1)} %refs_2_.1, f32[4,2048]{1,0:T(4,128)} %refs_3_.1, bf16[64,2048]{1,0:T(8,128)(2,1)} %bitcast.6, s32[4,128]{1,0:T(4,128)} %bitcast.7, ...), custom_call_target="tpu_custom_call" | custom-call | tf_op jit(solution)/shard_map/pallas_call | solution.py:999
  90.7 1.7 %copy.10 = bf16[128,1024]{1,0:T(8,128)(2,1)} copy(bf16[128,1024]{1,0:T(8,128)(2,1)} %shard_map.82) | data formatting | bytes 524288

commit v11 on v10

--- a/solution.py
+++ b/solution.py
@@ -179,7 +179,8 @@
         def _():
             z_copy(z, c, 1, src).start()
 
-    own_send(0)
+    yield lambda: own_send(0)
+
     for line in near_lines:
         meta_copy(line).start()
     for c in range(1, chunks):
@@ -511,7 +512,7 @@
 
 
 def front_kernel(
-    devices, start_weights,
+    devices, start_weights, send_first,
     sources, held, own_sem,
     normed, state, meta,
     window, queries, column, mixed, mine_out, their_out, sent_back, got_back, their_back,
@@ -882,11 +883,15 @@
         squares = squares + add_up(last, which)
     square = jnp.sum(squares, -1, keepdims=True)
     scale = lax.rsqrt(square / width + EPS)
-    for s in range(devices):
-        lanes = slice(s * shard, (s + 1) * shard)
+    step = width // 2 // CHUNKS
+    for i in range(2 * CHUNKS):
+        start = (part * CHUNKS + i) % (2 * CHUNKS) * step
+        lanes = pl.ds(pl.multiple_of(start, step), step)
         normed[:, lanes] = (
             state[:, lanes] * scale * (1.0 + modulation[2:3, lanes]) + modulation[1:2, lanes]
         ).astype(jnp.bfloat16)
+        if i == 0:
+            send_first()
     logits = lax.dot_general(
         router[...], normed[...], (((1,), (1,)), ((), ())), preferred_element_type=jnp.float32
     )
@@ -962,14 +967,15 @@
             same = (packed == (slot - inner) // SLOT * CAP + inner) & (inner < CAP)
             ref[...] = jnp.where(same, 1.0, 0.0).astype(jnp.bfloat16)
 
-    drain = front_kernel(
-        devices, start_weights, sources, held, own_sem, normed, state, meta,
-        *front_buffers, *front_sems,
-    )
-    expert_kernel(
+    experts = expert_kernel(
         devices, weight_copies, normed, meta, state, held[1], wide, out,
         *expert_buffers, *expert_sems,
     )
+    drain = front_kernel(
+        devices, start_weights, next(experts), sources, held, own_sem, normed, state, meta,
+        *front_buffers, *front_sems,
+    )
+    next(experts, None)
     drain()
 
 

time: 92.5 us -> 92.6 us (level)
  no operation moved by 1% of the time
where the time goes in v11:
time: 92.6 us; the launch traced here: 92.5 us
  Pallas kernels  90.8 us (98%)
  local copies, waits for them, and re-layouts  1.67 us (2%)
    pallas_call x1, Pallas kernels, block_call(): pl.pallas_call(functools.partial(block_kernel, devices), out_shape=jax.Sh...  90.8 us

profile of v11, /device:TPU:0, one launch (start us, length us, event | category | flops | bytes accessed | tf_op | source)
XLA Modules:
  0.0 92.5 jit_solution(4059837713847298954)
XLA Ops:
  0.0 90.8 %shard_map.82 = bf16[128,1024]{1,0:T(8,128)(2,1)} custom-call(bf16[128,2048]{1,0:T(8,128)(2,1)} %refs_0_.1, bf16[3,128,1024]{2,1,0:T(8,128)(2,1)} %bitcast.5, bf16[256,1024]{1,0:T(8,128)(2,1)} %refs_2_.1, f32[4,2048]{1,0:T(4,128)} %refs_3_.1, bf16[64,2048]{1,0:T(8,128)(2,1)} %bitcast.6, s32[4,128]{1,0:T(4,128)} %bitcast.7, ...), custom_call_target="tpu_custom_call" | custom-call | tf_op jit(solution)/shard_map/pallas_call | solution.py:1005
  90.8 1.7 %copy.10 = bf16[128,1024]{1,0:T(8,128)(2,1)} copy(bf16[128,1024]{1,0:T(8,128)(2,1)} %shard_map.82) | data formatting | bytes 524288
